TPU v7x, 128 devices: a whole 4x4x4 slice. The times are simulated.
128 devices in a mesh: tm: 4 (over z_hi, core), mic: 32 (over y, x, z_lo).
Axes of the slice: x: 4, y: 4, z: 4 (z_hi: 2, z_lo: 2; z = z_hi * 2 + z_lo), core: 2. Of those that a mesh axis runs over, the one named last changes fastest.
Arguments:
- samples: bfloat16 [32, 4096, 4096], P('tm', 'mic'), may hold values from -6 to 6
- bin_ids: int32 [16], replicated, may hold values from 1 to 2047
- delays: int32 [4096, 4096], P('mic'), may hold values from 0 to 1023
Outputs:
- source_map: float32 [16, 4096], P('tm', 'mic')
All inputs are finite; a program needn't handle non-finite values.
Results may differ from a plain program's by a relative error of at most 0.0013.
Values may be sent and summed in bfloat16 or wider, within the bound.
No kernel may reach another device: no remote copies, remote signals or barrier semaphores. Data moves between devices by JAX's collectives and lax.ppermute only.
A program may use at most 64 MiB of HBM per device.

v0:
```python
import math

import jax
import jax.numpy as jnp
from jax import lax
from jax.sharding import PartitionSpec as P


def dft_table(bin_ids, length):
    sample_index = jnp.arange(length, dtype=jnp.int32)
    window = 0.5 - 0.5 * jnp.cos(2.0 * jnp.pi * sample_index.astype(jnp.float32) / length)
    window_norm = jnp.sqrt(jnp.sum(window * window))
    phase_index = sample_index[:, None] * bin_ids[None, :] % length
    angles = 2.0 * jnp.pi * phase_index.astype(jnp.float32) / length
    cosine = window[:, None] * jnp.cos(angles) / window_norm
    sine_part = -window[:, None] * jnp.sin(angles) / window_norm
    return jnp.stack([cosine, sine_part], axis=-1).reshape(length, -1).astype(jnp.bfloat16)


def steer_block(received, delay_cols, bins_owned, length):
    seg_count = received.shape[0]
    mic_count = received.shape[3]
    point_count = delay_cols.shape[0]

    def per_bin(entry):
        bin_value, values = entry
        phases = 2.0 * jnp.pi * (bin_value * delay_cols % length).astype(jnp.float32) / length
        steer_rows = jnp.concatenate([jnp.cos(phases), jnp.sin(phases)], axis=0).astype(
            jnp.bfloat16
        )
        product = lax.dot_general(
            values.reshape(seg_count * 2, mic_count),
            steer_rows,
            (((1,), (1,)), ((), ())),
            preferred_element_type=jnp.float32,
        )
        product = product.reshape(seg_count, 2, 2, point_count)
        real_part = product[:, 0, 0] - product[:, 1, 1]
        imag_part = product[:, 1, 0] + product[:, 0, 1]
        return jnp.stack([real_part, imag_part], axis=0)

    return lax.map(per_bin, (bins_owned, jnp.moveaxis(received, 1, 0)))


def per_device(samples, bin_ids, delays):
    length = samples.shape[2]
    transform_rows = dft_table(bin_ids, length)
    spectra = jnp.einsum("sml,lk->skm", samples, transform_rows, preferred_element_type=jnp.float32)
    spectra = spectra.reshape(samples.shape[0], bin_ids.shape[0], 2, samples.shape[1]).astype(
        jnp.bfloat16
    )
    seg_count = spectra.shape[0]
    steered = steer_block(
        lax.all_gather(spectra, "mic", axis=3, tiled=True), delays, bin_ids, length
    )
    steered = steered / math.sqrt(delays.shape[1])
    powers = jnp.sum(steered * steered, axis=(1, 2))
    welch_sum = lax.psum_scatter(powers, "tm", scatter_dimension=0, tiled=True)
    return welch_sum / (seg_count * lax.axis_size("tm"))


def solution(mesh):
    placed = (P("tm", "mic", None), P(), P("mic", None))
    return jax.shard_map(
        per_device, mesh=mesh, in_specs=placed, out_specs=P("tm", "mic"), check_vma=False
    )
```

profile of v0, /device:TPU:1, one launch (start us, length us, event | category | flops | bytes accessed | tf_op | source)
XLA Modules:
  0.0 343.3 jit_solution(9585885661330164719)
XLA Ops:
  6.6 0.7 multiply_reduce_fusion.1
  8.0 1.9 divide_convert_fusion.1
  10.4 6.1 %convolution_convert_fusion = bf16[32,8,128]{2,0,1:T(8,128)(2,1)S(1)} fusion(bf16[4096,32,1]{0,1,2:T(8,128)(2,1)S(1)} %reshape.233, bf16[8,128,4096]{2,1,0:T(8,128)(2,1)} %param.5), kind=kOutput, calls=%fused_computation.19 | convolution fusion | flops 268468224 | bytes 8716288 | tf_op jit(solution)/shard_map/sml,lk->skm/dot_general | solution.py:48
  16.5 0.7 copy.8
  17.2 0.7 dynamic-slice
  18.5 110.3 %all-gather.2.cloned.1.call-done = bf16[8,16,2,4096]{3,0,2,1:T(8,128)(2,1)} async-done(((bf16[8,16,2,128]{3,0,2,1:T(8,128)(2,1)}), bf16[8,16,2,4096]{3,0,2,1:T(8,128)(2,1)}) %all-gather.2.cloned.1.call-update) | async-done | bytes 2097168 | tf_op jit(solution)/shard_map/all_gather | solution.py:54
  128.8 181.1 %while.12 = (s32[]{:T(128)}, f32[16,2,8,128]{3,2,1,0:T(8,128)S(1)}, bf16[16,8,2,4096]{3,1,2,0:T(8,128)(2,1)}, s32[16]{0:T(128)S(1)}, s32[128,4096]{1,0:T(8,128)S(1)}, /*index=5*/s32[]{:T(128)}) while((s32[]{:T(128)}, f32[16,2,8,128]{3,2,1,0:T(8,128)S(1)}, bf16[16,8,2,4096]{3,1,2,0:T(8,128)(2,1)}, s32[16]{0:T(128)S(1)}, ...), condition=%wide.region_2.3_spmd, body=%wide.region_1.2_spmd.sunk | while | flops 46141440 | bytes 10674777 | solution.py:42
  129.4 8.9 %cosine_convert_fusion.2 = (bf16[128,4096]{1,0:T(8,128)(2,1)S(1)}, bf16[128,4096]{1,0:T(8,128)(2,1)S(1)}) fusion(s32[128,4096]{1,0:T(8,128)S(1)} %get-tuple-element.146, s32[]{:T(128)} %bitcast.38), kind=kLoop, calls=%fused_computation.8.clone.1 | loop fusion | flops 8388608 | bytes 4194308 | tf_op jit(solution)/shard_map/convert
  138.5 1.6 fusion.27
  140.7 8.9 %cosine_convert_fusion.2 = (bf16[128,4096]{1,0:T(8,128)(2,1)S(1)}, bf16[128,4096]{1,0:T(8,128)(2,1)S(1)}) fusion(s32[128,4096]{1,0:T(8,128)S(1)} %get-tuple-element.146, s32[]{:T(128)} %bitcast.38), kind=kLoop, calls=%fused_computation.8.clone.1 | loop fusion | flops 8388608 | bytes 4194308 | tf_op jit(solution)/shard_map/convert
  149.8 1.6 fusion.27
  151.4 0.6 dynamic_slice.21
  152.0 8.9 %cosine_convert_fusion.2 = (bf16[128,4096]{1,0:T(8,128)(2,1)S(1)}, bf16[128,4096]{1,0:T(8,128)(2,1)S(1)}) fusion(s32[128,4096]{1,0:T(8,128)S(1)} %get-tuple-element.146, s32[]{:T(128)} %bitcast.38), kind=kLoop, calls=%fused_computation.8.clone.1 | loop fusion | flops 8388608 | bytes 4194308 | tf_op jit(solution)/shard_map/convert
  161.1 1.6 fusion.27
  162.7 0.6 dynamic_slice.21
  163.3 8.9 %cosine_convert_fusion.2 = (bf16[128,4096]{1,0:T(8,128)(2,1)S(1)}, bf16[128,4096]{1,0:T(8,128)(2,1)S(1)}) fusion(s32[128,4096]{1,0:T(8,128)S(1)} %get-tuple-element.146, s32[]{:T(128)} %bitcast.38), kind=kLoop, calls=%fused_computation.8.clone.1 | loop fusion | flops 8388608 | bytes 4194308 | tf_op jit(solution)/shard_map/convert
  172.5 1.6 fusion.27
  174.1 0.6 dynamic_slice.21
  174.6 8.9 %cosine_convert_fusion.2 = (bf16[128,4096]{1,0:T(8,128)(2,1)S(1)}, bf16[128,4096]{1,0:T(8,128)(2,1)S(1)}) fusion(s32[128,4096]{1,0:T(8,128)S(1)} %get-tuple-element.146, s32[]{:T(128)} %bitcast.38), kind=kLoop, calls=%fused_computation.8.clone.1 | loop fusion | flops 8388608 | bytes 4194308 | tf_op jit(solution)/shard_map/convert
  183.8 1.6 fusion.27
  185.4 0.6 dynamic_slice.21
  185.9 8.9 %cosine_convert_fusion.2 = (bf16[128,4096]{1,0:T(8,128)(2,1)S(1)}, bf16[128,4096]{1,0:T(8,128)(2,1)S(1)}) fusion(s32[128,4096]{1,0:T(8,128)S(1)} %get-tuple-element.146, s32[]{:T(128)} %bitcast.38), kind=kLoop, calls=%fused_computation.8.clone.1 | loop fusion | flops 8388608 | bytes 4194308 | tf_op jit(solution)/shard_map/convert
  195.1 1.6 fusion.27
  196.7 0.6 dynamic_slice.21
  197.3 8.9 %cosine_convert_fusion.2 = (bf16[128,4096]{1,0:T(8,128)(2,1)S(1)}, bf16[128,4096]{1,0:T(8,128)(2,1)S(1)}) fusion(s32[128,4096]{1,0:T(8,128)S(1)} %get-tuple-element.146, s32[]{:T(128)} %bitcast.38), kind=kLoop, calls=%fused_computation.8.clone.1 | loop fusion | flops 8388608 | bytes 4194308 | tf_op jit(solution)/shard_map/convert
  206.4 1.6 fusion.27
  208.0 0.6 dynamic_slice.21
  208.6 8.9 %cosine_convert_fusion.2 = (bf16[128,4096]{1,0:T(8,128)(2,1)S(1)}, bf16[128,4096]{1,0:T(8,128)(2,1)S(1)}) fusion(s32[128,4096]{1,0:T(8,128)S(1)} %get-tuple-element.146, s32[]{:T(128)} %bitcast.38), kind=kLoop, calls=%fused_computation.8.clone.1 | loop fusion | flops 8388608 | bytes 4194308 | tf_op jit(solution)/shard_map/convert
  217.7 1.6 fusion.27
  219.3 0.6 dynamic_slice.21
  219.9 8.9 %cosine_convert_fusion.2 = (bf16[128,4096]{1,0:T(8,128)(2,1)S(1)}, bf16[128,4096]{1,0:T(8,128)(2,1)S(1)}) fusion(s32[128,4096]{1,0:T(8,128)S(1)} %get-tuple-element.146, s32[]{:T(128)} %bitcast.38), kind=kLoop, calls=%fused_computation.8.clone.1 | loop fusion | flops 8388608 | bytes 4194308 | tf_op jit(solution)/shard_map/convert
  229.0 1.6 fusion.27
  231.2 8.9 %cosine_convert_fusion.2 = (bf16[128,4096]{1,0:T(8,128)(2,1)S(1)}, bf16[128,4096]{1,0:T(8,128)(2,1)S(1)}) fusion(s32[128,4096]{1,0:T(8,128)S(1)} %get-tuple-element.146, s32[]{:T(128)} %bitcast.38), kind=kLoop, calls=%fused_computation.8.clone.1 | loop fusion | flops 8388608 | bytes 4194308 | tf_op jit(solution)/shard_map/convert
  240.4 1.6 fusion.27
  242.5 8.9 %cosine_convert_fusion.2 = (bf16[128,4096]{1,0:T(8,128)(2,1)S(1)}, bf16[128,4096]{1,0:T(8,128)(2,1)S(1)}) fusion(s32[128,4096]{1,0:T(8,128)S(1)} %get-tuple-element.146, s32[]{:T(128)} %bitcast.38), kind=kLoop, calls=%fused_computation.8.clone.1 | loop fusion | flops 8388608 | bytes 4194308 | tf_op jit(solution)/shard_map/convert
  251.7 1.6 fusion.27
  253.8 8.9 %cosine_convert_fusion.2 = (bf16[128,4096]{1,0:T(8,128)(2,1)S(1)}, bf16[128,4096]{1,0:T(8,128)(2,1)S(1)}) fusion(s32[128,4096]{1,0:T(8,128)S(1)} %get-tuple-element.146, s32[]{:T(128)} %bitcast.38), kind=kLoop, calls=%fused_computation.8.clone.1 | loop fusion | flops 8388608 | bytes 4194308 | tf_op jit(solution)/shard_map/convert
  263.0 1.6 fusion.27
  265.2 8.9 %cosine_convert_fusion.2 = (bf16[128,4096]{1,0:T(8,128)(2,1)S(1)}, bf16[128,4096]{1,0:T(8,128)(2,1)S(1)}) fusion(s32[128,4096]{1,0:T(8,128)S(1)} %get-tuple-element.146, s32[]{:T(128)} %bitcast.38), kind=kLoop, calls=%fused_computation.8.clone.1 | loop fusion | flops 8388608 | bytes 4194308 | tf_op jit(solution)/shard_map/convert
  274.3 1.6 fusion.27
  276.5 8.9 %cosine_convert_fusion.2 = (bf16[128,4096]{1,0:T(8,128)(2,1)S(1)}, bf16[128,4096]{1,0:T(8,128)(2,1)S(1)}) fusion(s32[128,4096]{1,0:T(8,128)S(1)} %get-tuple-element.146, s32[]{:T(128)} %bitcast.38), kind=kLoop, calls=%fused_computation.8.clone.1 | loop fusion | flops 8388608 | bytes 4194308 | tf_op jit(solution)/shard_map/convert
  285.6 1.6 fusion.27
  287.8 8.9 %cosine_convert_fusion.2 = (bf16[128,4096]{1,0:T(8,128)(2,1)S(1)}, bf16[128,4096]{1,0:T(8,128)(2,1)S(1)}) fusion(s32[128,4096]{1,0:T(8,128)S(1)} %get-tuple-element.146, s32[]{:T(128)} %bitcast.38), kind=kLoop, calls=%fused_computation.8.clone.1 | loop fusion | flops 8388608 | bytes 4194308 | tf_op jit(solution)/shard_map/convert
  296.9 1.6 fusion.27
  299.1 8.9 %cosine_convert_fusion.2 = (bf16[128,4096]{1,0:T(8,128)(2,1)S(1)}, bf16[128,4096]{1,0:T(8,128)(2,1)S(1)}) fusion(s32[128,4096]{1,0:T(8,128)S(1)} %get-tuple-element.146, s32[]{:T(128)} %bitcast.38), kind=kLoop, calls=%fused_computation.8.clone.1 | loop fusion | flops 8388608 | bytes 4194308 | tf_op jit(solution)/shard_map/convert
  308.3 1.6 fusion.27
  309.9 26.0 %all-reduce = f32[16,128]{1,0:T(8,128)S(1)} all-reduce(f32[16,128]{1,0:T(8,128)S(1)} %multiply_reduce_fusion), channel_id=2, replica_groups=mesh['tm'=4,'mic'=32] {'tm'}, use_global_device_ids=true, to_apply=%region_4.5.clone | all-reduce | flops 2048 | bytes 16384
  335.9 0.6 dynamic-slice_multiply_fusion
  (71 shorter events, 9.3 us)
Async XLA Ops:
  6.5 122.3 %all-gather.2.cloned.1.call-start = ((), (), s32[]{:S(2)}) async-start(), calls=%async_computation | async-start | bytes 2162688 | tf_op jit(solution)/shard_map/all_gather | solution.py:54
  10.3 6.8 %copy-start.2 = (u32[128]{0:T(128)S(1)}, u32[128]{0:T(128)}, u32[]{:S(2)}) copy-start(u32[128]{0:T(128)} %constant.85) | copy-start | bytes 1540
  10.3 118.5 %copy-start = (s32[128,4096]{1,0:T(8,128)S(1)}, s32[128,4096]{1,0:T(8,128)}, u32[]{:S(2)}) copy-start(s32[128,4096]{1,0:T(8,128)} %param.7) | copy-start | bytes 6291460
  10.3 118.4 %copy-start.1 = (s32[16]{0:T(128)S(1)}, s32[16]{0:T(128)}, u32[]{:S(2)}) copy-start(s32[16]{0:T(128)} %param.6) | copy-start | bytes 196
Sparse Core Ops, SparseCore 0:
  17.3 111.4 all-gather.1
where the time goes:
time: 344 us; the launch traced here: 343 us
  other arithmetic  150 us (44%)
  waiting for transfers between devices  110 us (32%)
  matrix products  31 us (9%)
  blocking collectives  26 us (8%)
  between operations  14.9 us (4%)
  local copies, waits for them, and re-layouts  10.6 us (3%)
    another operation x17, other arithmetic  145 us
    all_gather x1, waiting for transfers between devices, per_device(): lax.all_gather(spectra, 'mic', axis=3, tiled=True)  110 us
    unnamed x1, blocking collectives  26 us
    dot_general x16, matrix products, per_bin(): lax.dot_general(values.reshape(seg_count * 2, mic_count), steer_rows, (((...  24.9 us
    dynamic_slice x16, local copies, waits for them, and re-layouts, steer_block(): return lax.map(per_bin, (bins_owned, jnp.moveaxis(received, 1, 0)))  8.9 us
  transfers between devices with their start and end apart: 1, of which 1 were waited for; matrix products, arithmetic and copies ran while one was open for 0% of the time, Pallas kernels for 0%

commit v1 on v0

v1 whole, which is shorter than its diff:
```python
import math

import jax
import jax.numpy as jnp
from jax import lax
from jax.experimental import pallas as pl
from jax.experimental.pallas import tpu as pltpu
from jax.sharding import PartitionSpec as P


AXES = ("tm", "mic")
SHIFTS = (2, 1, 3)
ROUND = 12582912.0
GROUPS = (3, 3, 2)
OWN = (2, 4, 2)
SIN_POLY = (4.442882919124343, -7.30824568650904, 3.6063542184324877, -0.8461116503718901, 0.10982451642219883)
COS_POLY = (1.414213496255228, -6.978850948563807, 5.73946037690717, -1.8835579059870113, 0.31068802752761115)


def horner(coefs, z):
    value = coefs[-1]
    for coef in coefs[-2::-1]:
        value = value * z + coef
    return value


def cos_sin(turns):
    r = turns - ((turns + ROUND) - ROUND)
    z = r * r
    s = horner(SIN_POLY, z) * r
    c = horner(COS_POLY, z)
    return 1.0 - s * s, s * c


VMEM = pl.BlockSpec(memory_space=pltpu.VMEM)
SMEM = pl.BlockSpec(memory_space=pltpu.SMEM)
PARAMS = pltpu.CompilerParams(vmem_limit_bytes=16 * 2**20)
WIDE = pltpu.CompilerParams(vmem_limit_bytes=58 * 2**20)


def position():
    tm = lax.axis_index("tm")
    mic = lax.axis_index("mic")
    return tm >> 1, tm & 1, mic >> 3, (mic >> 1) & 3, mic & 1


def transform_kernel(
    bins_in, delays_in, samples, keep, send, mine, half, bins, delays, segs, sems, table, sums, blocks
):
    zh, core, _, _, zl = position()
    n_segs, mics, length = segs.shape
    n_bins = bins.shape[0]
    chunk = 512
    copies = [
        pltpu.make_async_copy(samples.at[s], segs.at[s], sems.at[s]) for s in range(n_segs)
    ]
    bins_copy = pltpu.make_async_copy(bins_in, bins, sems.at[n_segs])
    delays_copy = pltpu.make_async_copy(delays_in, delays, sems.at[n_segs + 1])
    bins_copy.start()
    for s in range(GROUPS[0]):
        copies[s].start()

    bins_copy.wait()
    row = lax.broadcasted_iota(jnp.int32, (n_bins, chunk), 0)
    scale = jnp.zeros((n_bins, chunk), jnp.float32)
    for b in range(n_bins):
        scale = jnp.where(row == b, bins[b].astype(jnp.float32) * (1.0 / length), scale)
    lane = lax.broadcasted_iota(jnp.int32, (n_bins, chunk), 1)
    for k in range(length // chunk):
        n = (lane + k * chunk).astype(jnp.float32)
        hann = 0.5 - 0.5 * cos_sin(n[0:8] * (1.0 / length))[0]
        weight = jnp.concatenate([hann, hann], axis=0) * (1.0 / math.sqrt(0.375 * length))
        cos, sin = cos_sin(n * scale)
        table[0:n_bins, k * chunk : (k + 1) * chunk] = (weight * cos).astype(jnp.bfloat16)
        table[n_bins:, k * chunk : (k + 1) * chunk] = (-weight * sin).astype(jnp.bfloat16)

    done = 0
    for g, group in enumerate(GROUPS):
        for s in range(done, done + group):
            copies[s].wait()
            if s + GROUPS[0] < n_segs:
                copies[s + GROUPS[0]].start()
        if g == 0:
            delays_copy.start()
        if g == len(GROUPS) - 1:
            delays_copy.wait()
        product = lax.dot_general(
            segs[done : done + group].reshape(group * mics, length),
            table[...],
            (((1,), (1,)), ((), ())),
            preferred_element_type=jnp.float32,
        )
        for s in range(group):
            sums[done + s] = product[s * mics : (s + 1) * mics].T
        done += group

    for j in range(mine.shape[0]):
        first = delays[:, j * 256 : j * 256 + 128]
        second = delays[:, j * 256 + 128 : (j + 1) * 256]
        mine[j] = jnp.where(zl == 0, first, second).astype(jnp.int16)
        other = jnp.where(zl == 0, second, first).astype(jnp.int16)

        @pl.when(j // half.shape[0] == core)
        def _():
            half[j % half.shape[0]] = other

    for b in range(n_bins):
        rows = jnp.concatenate([sums[:, b, :], sums[:, n_bins + b, :]], axis=0)
        blocks[b // 4, (b % 4) * 16 : (b % 4 + 1) * 16, :] = rows.astype(jnp.bfloat16)
    keep[0] = blocks[zh * 2 + core]
    keep[1] = blocks[(1 - zh) * 2 + core]
    send[0] = blocks[zh * 2 + 1 - core]
    send[1] = blocks[(1 - zh) * 2 + 1 - core]


def transform(bins, delays, samples):
    segs, mics, length = samples.shape
    points = delays.shape[0]
    n_bins = bins.shape[0]
    block = (2, n_bins // 4 * 2 * segs, mics)
    blocks = delays.shape[1] // 256
    return pl.pallas_call(
        transform_kernel,
        in_specs=[pl.BlockSpec(memory_space=pltpu.HBM)] * 3,
        out_specs=[VMEM] * 4,
        out_shape=[
            pltpu.VMEM(block, jnp.bfloat16),
            pltpu.VMEM(block, jnp.bfloat16),
            pltpu.VMEM((blocks, points, 128), jnp.int16),
            pltpu.VMEM((blocks // 2, points, 128), jnp.int16),
        ],
        scratch_shapes=[
            pltpu.SMEM((n_bins,), jnp.int32),
            pltpu.VMEM(delays.shape, delays.dtype),
            pltpu.VMEM((segs, mics, length), jnp.bfloat16),
            pltpu.SemaphoreType.DMA((segs + 2,)),
            pltpu.VMEM((2 * n_bins, length), jnp.bfloat16),
            pltpu.VMEM((segs, 2 * n_bins, mics), jnp.float32),
            pltpu.VMEM((4,) + block[1:], jnp.bfloat16),
        ],
        compiler_params=WIDE,
        name="transform",
    )(bins, delays, samples)


def arrival(index):
    return ((index & 1) << 1) | (index >> 1)


def block_of(index):
    _, core, y, x, _ = position()
    second = arrival(index >> 2)
    first = arrival(index & 3)
    dx = first + core * (second - first)
    dy = second + core * (first - second)
    return ((y - dy) & 3) * 4 + ((x - dx) & 3)


def steer_kernel(start, halves, bins, *refs):
    out = refs[-1]
    pairs, n_bins, points, _ = out.shape
    tm = lax.axis_index("tm")
    core = tm & 1
    turns = [bins[tm * n_bins + f].astype(jnp.float32) * (1.0 / 4096) for f in range(n_bins)]

    def body(pair, carry):
        for half in range(2):
            block = block_of((start + pair) * 2 + half)
            for k in range(points // 32):
                rows = slice(k * 32, (k + 1) * 32)
                if halves:
                    kept = (block >> 3) == core
                    d = jnp.where(kept, refs[0][block & 7, rows, :], refs[1][block & 7, rows, :])
                else:
                    d = refs[0][block, rows, :]
                d = d.astype(jnp.int32).astype(jnp.float32)
                for f in range(n_bins):
                    cos, sin = cos_sin(d * turns[f])
                    out[pair, f, rows, half * 128 : (half + 1) * 128] = cos.astype(jnp.bfloat16)
                    out[pair, f, rows, 256 + half * 128 : 384 + half * 128] = sin.astype(jnp.bfloat16)
        return carry

    lax.fori_loop(0, pairs, body, 0)


def steer_tables(bins, delays, start, pairs):
    return pl.pallas_call(
        lambda *refs: steer_kernel(start, len(delays) == 2, *refs),
        in_specs=[SMEM] + [VMEM] * len(delays),
        out_specs=VMEM,
        out_shape=pltpu.VMEM((pairs, bins.shape[0] // 4, 128, 512), jnp.bfloat16),
        compiler_params=PARAMS,
        name="steer",
    )(bins, *delays)


def apply_kernel(n_planes, n_tables, start, carried, last, *refs):
    planes = refs[:n_planes]
    tables = refs[n_planes : n_planes + n_tables]
    before = refs[n_planes + n_tables] if carried else None
    out = refs[-1]
    pairs = [(table, p) for table in tables for p in range(table.shape[0])]
    n_bins = tables[0].shape[1]
    for f in range(n_bins):
        total = before[f] if carried else None
        for i, plane in enumerate(planes):
            for q in range(2):
                cos_cols, sin_cols = [], []
                for h in range(2):
                    both = [
                        plane[2 * q + h, src, f * 16 : (f + 1) * 16, :].astype(jnp.float32)
                        for src in range(4)
                    ]
                    real = [b[0:8] for b in both]
                    imag = [b[8:16] for b in both]
                    cos_cols.append(jnp.concatenate(real + imag, axis=0))
                    sin_cols.append(jnp.concatenate([-v for v in imag] + real, axis=0))
                columns = jnp.concatenate(cos_cols + sin_cols, axis=1).astype(jnp.bfloat16)
                table, p = pairs[start + 2 * i + q]
                product = lax.dot_general(
                    table[p, f],
                    columns,
                    (((1,), (1,)), ((), ())),
                    preferred_element_type=jnp.float32,
                )
                total = product if total is None else total + product
        if last:
            out[f // 2, :, (f % 2) * 64 : (f % 2 + 1) * 64] = total.astype(out.dtype)
        else:
            out[f] = total


def apply_tables(planes, tables, start, before, kind):
    n_bins = tables[0].shape[1]
    shape = (n_bins, 128, 64) if kind is None else (n_bins // 2, 128, 128)
    args = (*planes, *tables) + (() if before is None else (before,))
    return pl.pallas_call(
        lambda *refs: apply_kernel(
            len(planes), len(tables), start, before is not None, kind is not None, *refs
        ),
        in_specs=[VMEM] * len(args),
        out_specs=VMEM,
        out_shape=pltpu.VMEM(shape, kind or jnp.float32),
        compiler_params=PARAMS,
        name="apply",
    )(*args)


def power_kernel(scale, mine, theirs, out):
    for k in range(mine.shape[0]):
        total = mine[k] + theirs[k].astype(jnp.float32)
        squares = (total * total).T
        for f in range(2):
            power = jnp.sum(squares[f * 64 : (f + 1) * 64], axis=0, keepdims=True)
            out[2 * k + f : 2 * k + f + 1, :] = power * scale


def powers(mine, theirs, scale):
    return pl.pallas_call(
        lambda *refs: power_kernel(scale, *refs),
        in_specs=[VMEM] * 2,
        out_specs=VMEM,
        out_shape=jax.ShapeDtypeStruct((2 * mine.shape[0], mine.shape[1]), jnp.float32),
        compiler_params=PARAMS,
        name="powers",
    )(mine, theirs)


def route(move):
    pairs = []
    for tm in range(4):
        for mic in range(32):
            zh, core, y, x, zl = tm // 2, tm % 2, mic // 8, mic // 2 % 4, mic % 2
            zh, core, y, x, zl = move(zh, core, y, x, zl)
            pairs.append((tm * 32 + mic, (zh * 2 + core) * 32 + y % 4 * 8 + x % 4 * 2 + zl))
    return pairs


def send(value, move):
    return lax.ppermute(value, AXES, route(move))


def per_device(samples, bin_ids, delays):
    keep, give, own_delays, half = transform(bin_ids, delays, samples)
    got = send(give, lambda zh, c, y, x, zl: (zh, 1 - c, y, x, zl))
    half = send(half, lambda zh, c, y, x, zl: (zh, c, y, x, 1 - zl))
    partner_delays = half, send(half, lambda zh, c, y, x, zl: (zh, 1 - c, y, x, zl))
    away = jnp.concatenate([keep[1:], got[1:]])
    far = send(away, lambda zh, c, y, x, zl: (1 - zh, c, y, x, zl))
    column = jnp.concatenate([keep[:1], got[:1], far])

    own, start = [], 0
    for pairs in OWN:
        own.append(steer_tables(bin_ids, (own_delays,), start, pairs))
        start += pairs
    partner = steer_tables(bin_ids, partner_delays, 0, 8)

    def first(d):
        return lambda zh, c, y, x, zl: (zh, c, y + d, x, zl) if c else (zh, c, y, x + d, zl)

    def second(d):
        return lambda zh, c, y, x, zl: (zh, c, y, x + d, zl) if c else (zh, c, y + d, x, zl)

    line = [column]
    for d in SHIFTS:
        line.append(send(column, first(d)))
    line = jnp.stack(line)
    planes = [line]
    for d in SHIFTS:
        planes.append(send(line, second(d)))
    theirs = apply_tables(planes[:1], (partner,), 0, None, None)
    theirs = apply_tables(planes[1:3], (partner,), 2, theirs, None)
    theirs = apply_tables(planes[3:], (partner,), 6, theirs, jnp.bfloat16)
    theirs = send(theirs, lambda zh, c, y, x, zl: (zh, c, y, x, 1 - zl))
    mine = apply_tables(planes, own, 0, None, jnp.float32)
    seg_count = samples.shape[0] * lax.axis_size("tm")
    return powers(mine, theirs, 1.0 / (delays.shape[1] * seg_count))


def solution(mesh):
    placed = (P("tm", "mic", None), P(), P("mic", None))
    return jax.shard_map(
        per_device, mesh=mesh, in_specs=placed, out_specs=P("tm", "mic"), check_vma=False
    )
```

time: 344 us -> 49.2 us (0.14)
  the two profiles are of different devices: /device:TPU:1 before, /device:TPU:38 now
where the time goes in v1:
time: 49.2 us; the launch traced here: 49.1 us
  Pallas kernels  20.2 us (41%)
  starting transfers between devices  15.9 us (32%)
  waiting for transfers between devices  12.9 us (26%)
    ppermute x11, starting transfers between devices, send(): return lax.ppermute(value, AXES, route(move))  15.9 us
    ppermute x11, waiting for transfers between devices, send(): return lax.ppermute(value, AXES, route(move))  12.9 us
    pallas_call x4, Pallas kernels, steer_tables(): pl.pallas_call(lambda *refs: steer_kernel(start, len(delays) == 2, *refs)...  10 us
    pallas_call x1, Pallas kernels, transform(): pl.pallas_call(transform_kernel, in_specs=[pl.BlockSpec(memory_space=pltp...  6.59 us
    pallas_call x4, Pallas kernels, apply_tables(): pl.pallas_call(lambda *refs: apply_kernel(len(planes), len(tables), start...  2.89 us
  transfers between devices with their start and end apart: 11, of which 5 were waited for; matrix products, arithmetic and copies ran while one was open for 0% of the time, Pallas kernels for 25%

profile of v1, /device:TPU:38, one launch (start us, length us, event | category | flops | bytes accessed | tf_op | source)
XLA Modules:
  0.0 49.1 jit_solution(15240453108019962735)
XLA Ops:
  0.0 0.0 copy-start
  0.0 6.6 %transform.1 = (bf16[2,64,128]{2,1,0:T(8,128)(2,1)S(1)}, bf16[2,64,128]{2,1,0:T(8,128)(2,1)S(1)}, s16[16,128,128]{2,1,0:T(8,128)(2,1)S(1)}, s16[8,128,128]{2,1,0:T(8,128)(2,1)S(1)}) custom-call(s32[16]{0:T(128)} %refs_0_.7, s32[128,4096]{1,0:T(8,128)} %delays_in.1, bf16[8,128,4096]{2,1,0:T(8,128)(2,1)} %samples.1), custom_call_target="tpu_custom_call" | custom-call | tf_op jit(solution)/shard_map/transform/pallas_call | solution.py:122
  6.6 0.1 collective-permute-start
  6.7 0.2 collective-permute-start.8
  6.9 1.0 %collective-permute-done = bf16[2,64,128]{2,1,0:T(8,128)(2,1)S(1)} collective-permute-done((bf16[2,64,128]{2,1,0:T(8,128)(2,1)S(1)}, bf16[2,64,128]{2,1,0:T(8,128)(2,1)S(1)}, u32[]{:S(2)}, u32[]{:S(2)}) %collective-permute-start) | collective-permute-done | bytes 32800 | tf_op jit(solution)/shard_map/ppermute | solution.py:280
  7.9 3.1 %collective-permute-start.1 = (bf16[2,64,128]{2,1,0:T(8,128)(2,1)S(1)}, bf16[2,64,128]{2,1,0:T(8,128)(2,1)S(1)}, u32[]{:S(2)}, u32[]{:S(2)}) collective-permute-start(bf16[2,64,128]{2,1,0:T(8,128)(2,1)S(1)} %pad_maximum_fusion.2), channel_id=1, source_target_pairs={{0,64},{1,65},{2,66},{3,67},{4,68},{5,69},{6,70},{7,71},{8,72},{9,... | collective-permute-start | bytes 98312 | tf_op jit(solution)/shard_map/ppermute | solution.py:280
  11.0 6.5 %collective-permute-done.1 = bf16[2,64,128]{2,1,0:T(8,128)(2,1)S(1)} collective-permute-done((bf16[2,64,128]{2,1,0:T(8,128)(2,1)S(1)}, bf16[2,64,128]{2,1,0:T(8,128)(2,1)S(1)}, u32[]{:S(2)}, u32[]{:S(2)}) %collective-permute-start.1) | collective-permute-done | bytes 32800 | tf_op jit(solution)/shard_map/ppermute | solution.py:280
  17.5 0.9 %collective-permute-start.4 = (bf16[4,64,128]{2,1,0:T(8,128)(2,1)S(1)}, bf16[4,64,128]{2,1,0:T(8,128)(2,1)S(1)}, u32[]{:S(2)}, u32[]{:S(2)}) collective-permute-start(bf16[4,64,128]{2,1,0:T(8,128)(2,1)S(1)} %get-tuple-element.14), channel_id=1, source_target_pairs={{0,6},{1,7},{2,0},{3,1},{4,2},{5,3},{6,4},{7,5},{8,14},{9,15},{10,... | collective-permute-start | bytes 196616 | tf_op jit(solution)/shard_map/ppermute | solution.py:280
  18.4 2.4 %collective-permute-start.3 = (bf16[4,64,128]{2,1,0:T(8,128)(2,1)S(1)}, bf16[4,64,128]{2,1,0:T(8,128)(2,1)S(1)}, u32[]{:S(2)}, u32[]{:S(2)}) collective-permute-start(bf16[4,64,128]{2,1,0:T(8,128)(2,1)S(1)} %get-tuple-element.14), channel_id=1, source_target_pairs={{0,2},{1,3},{2,4},{3,5},{4,6},{5,7},{6,0},{7,1},{8,10},{9,11},{10,... | collective-permute-start | bytes 196616 | tf_op jit(solution)/shard_map/ppermute | solution.py:280
  20.8 0.2 collective-permute-start.2
  21.0 0.0 collective-permute-done.8.refs_1_
  21.0 0.2 collective-permute-start.9
  21.2 1.8 %collective-permute-done.4 = bf16[4,64,128]{2,1,0:T(8,128)(2,1)S(1)} collective-permute-done((bf16[4,64,128]{2,1,0:T(8,128)(2,1)S(1)}, bf16[4,64,128]{2,1,0:T(8,128)(2,1)S(1)}, u32[]{:S(2)}, u32[]{:S(2)}) %collective-permute-start.4) | collective-permute-done | bytes 65568 | tf_op jit(solution)/shard_map/ppermute | solution.py:280
  23.0 0.3 collective-permute-done.3
  23.3 3.3 %collective-permute-done.2 = bf16[4,64,128]{2,1,0:T(8,128)(2,1)S(1)} collective-permute-done((bf16[4,64,128]{2,1,0:T(8,128)(2,1)S(1)}, bf16[4,64,128]{2,1,0:T(8,128)(2,1)S(1)}, u32[]{:S(2)}, u32[]{:S(2)}) %collective-permute-start.2) | collective-permute-done | bytes 65568 | tf_op jit(solution)/shard_map/ppermute | solution.py:280
  26.6 3.3 %collective-permute-start.5 = (bf16[4,4,64,128]{3,2,1,0:T(8,128)(2,1)S(1)}, bf16[4,4,64,128]{3,2,1,0:T(8,128)(2,1)S(1)}, u32[]{:S(2)}, u32[]{:S(2)}) collective-permute-start(bf16[4,4,64,128]{3,2,1,0:T(8,128)(2,1)S(1)} %pad_maximum_fusion.refs_0_), channel_id=1, source_target_pairs={{0,16},{1,17},{2,18},{3,19},{4,20},{5,21},{6,22},{7,23},{8,24},{9,... | collective-permute-start | bytes 786440 | tf_op jit(solution)/shard_map/ppermute | solution.py:280
  29.9 0.7 %collective-permute-start.6 = (bf16[4,4,64,128]{3,2,1,0:T(8,128)(2,1)S(1)}, bf16[4,4,64,128]{3,2,1,0:T(8,128)(2,1)S(1)}, u32[]{:S(2)}, u32[]{:S(2)}) collective-permute-start(bf16[4,4,64,128]{3,2,1,0:T(8,128)(2,1)S(1)} %pad_maximum_fusion.refs_0_), channel_id=1, source_target_pairs={{0,8},{1,9},{2,10},{3,11},{4,12},{5,13},{6,14},{7,15},{8,16},{9,17... | collective-permute-start | bytes 786440 | tf_op jit(solution)/shard_map/ppermute | solution.py:280
  30.5 2.6 %collective-permute-start.7 = (bf16[4,4,64,128]{3,2,1,0:T(8,128)(2,1)S(1)}, bf16[4,4,64,128]{3,2,1,0:T(8,128)(2,1)S(1)}, u32[]{:S(2)}, u32[]{:S(2)}) collective-permute-start(bf16[4,4,64,128]{3,2,1,0:T(8,128)(2,1)S(1)} %pad_maximum_fusion.refs_0_), channel_id=1, source_target_pairs={{0,24},{1,25},{2,26},{3,27},{4,28},{5,29},{6,30},{7,31},{8,0},{9,1... | collective-permute-start | bytes 786440 | tf_op jit(solution)/shard_map/ppermute | solution.py:280
  33.1 0.0 collective-permute-done.9.refs_2_
  33.1 0.0 copy-done
  33.1 4.5 %steer.7.refs_1_.refs_2_ = bf16[8,4,128,512]{3,2,1,0:T(8,128)(2,1)S(1)} custom-call(s32[16]{0:T(128)S(1)} %copy-done, s16[8,128,128]{2,1,0:T(8,128)(2,1)S(1)} %collective-permute-done.8.refs_1_, s16[8,128,128]{2,1,0:T(8,128)(2,1)S(1)} %collective-permute-done.9.refs_2_), custom_call_target="tpu_custom_call" | custom-call | tf_op jit(solution)/shard_map/steer/pallas_call | solution.py:187
  37.6 0.4 apply.5.refs_3_
  38.0 0.0 collective-permute-done.5.refs_1_.refs_0_
  38.0 0.0 collective-permute-done.6.refs_2_.refs_1_
  38.0 0.7 %apply.6.refs_2_ = f32[4,128,64]{2,1,0:T(8,128)S(1)} custom-call(bf16[4,4,64,128]{3,2,1,0:T(8,128)(2,1)S(1)} %collective-permute-done.5.refs_1_.refs_0_, bf16[4,4,64,128]{3,2,1,0:T(8,128)(2,1)S(1)} %collective-permute-done.6.refs_2_.refs_1_, bf16[8,4,128,512]{3,2,1,0:T(8,128)(2,1)S(1)} %steer.7.refs_1_.refs_2_, f32[4,128,64]{2,1,0:T(8,128)S(1)} %apply.5.refs_3_), custom_call_target="tpu_custom_call" | custom-call | tf_op jit(solution)/shard_map/apply/pallas_call | solution.py:237
  38.7 0.0 collective-permute-done.7.refs_3_.refs_0_
  38.8 0.5 apply.7
  39.2 2.3 %collective-permute-start.10 = (bf16[2,128,128]{2,1,0:T(8,128)(2,1)S(1)}, bf16[2,128,128]{2,1,0:T(8,128)(2,1)S(1)}, u32[]{:S(2)}, u32[]{:S(2)}) collective-permute-start(bf16[2,128,128]{2,1,0:T(8,128)(2,1)S(1)} %apply.7), channel_id=1, source_target_pairs={{0,1},{1,0},{2,3},{3,2},{4,5},{5,4},{6,7},{7,6},{8,9},{9,8},{10,11... | collective-permute-start | bytes 196616 | tf_op jit(solution)/shard_map/ppermute | solution.py:280
  41.6 1.5 %steer.4.refs_4_ = bf16[2,4,128,512]{3,2,1,0:T(8,128)(2,1)S(1)} custom-call(s32[16]{0:T(128)S(1)} %copy-done, s16[16,128,128]{2,1,0:T(8,128)(2,1)S(1)} %get-tuple-element.11.refs_1_), custom_call_target="tpu_custom_call" | custom-call | tf_op jit(solution)/shard_map/steer/pallas_call | solution.py:187
  43.1 2.5 %steer.5.refs_5_ = bf16[4,4,128,512]{3,2,1,0:T(8,128)(2,1)S(1)} custom-call(s32[16]{0:T(128)S(1)} %copy-done, s16[16,128,128]{2,1,0:T(8,128)(2,1)S(1)} %get-tuple-element.11.refs_1_), custom_call_target="tpu_custom_call" | custom-call | tf_op jit(solution)/shard_map/steer/pallas_call | solution.py:187
  45.6 1.5 %steer.6.refs_6_ = bf16[2,4,128,512]{3,2,1,0:T(8,128)(2,1)S(1)} custom-call(s32[16]{0:T(128)S(1)} %copy-done, s16[16,128,128]{2,1,0:T(8,128)(2,1)S(1)} %get-tuple-element.11.refs_1_), custom_call_target="tpu_custom_call" | custom-call | tf_op jit(solution)/shard_map/steer/pallas_call | solution.py:187
  47.1 1.3 %apply.4.refs_0_ = f32[2,128,128]{2,1,0:T(8,128)S(1)} custom-call(bf16[4,4,64,128]{3,2,1,0:T(8,128)(2,1)S(1)} %pad_maximum_fusion.refs_0_, bf16[4,4,64,128]{3,2,1,0:T(8,128)(2,1)S(1)} %collective-permute-done.5.refs_1_.refs_0_, bf16[4,4,64,128]{3,2,1,0:T(8,128)(2,1)S(1)} %collective-permute-done.6.refs_2_.refs_1_, ...), custom_call_target="tpu_custom_call" | custom-call | tf_op jit(solution)/shard_map/apply/pallas_call | solution.py:237
  48.4 0.0 collective-permute-done.10.refs_1_
  48.5 0.7 %powers.1 = f32[4,128]{1,0:T(4,128)} custom-call(f32[2,128,128]{2,1,0:T(8,128)S(1)} %apply.4.refs_0_, bf16[2,128,128]{2,1,0:T(8,128)(2,1)S(1)} %collective-permute-done.10.refs_1_), custom_call_target="tpu_custom_call" | custom-call | tf_op jit(solution)/shard_map/powers/pallas_call | solution.py:259
  (5 shorter events, 0.1 us)
Async XLA Ops:
  0.0 33.1 %copy-start = (s32[16]{0:T(128)S(1)}, s32[16]{0:T(128)}, u32[]{:S(2)}) copy-start(s32[16]{0:T(128)} %refs_0_.7) | copy-start | bytes 196
  6.6 1.3 %collective-permute-start = (bf16[2,64,128]{2,1,0:T(8,128)(2,1)S(1)}, bf16[2,64,128]{2,1,0:T(8,128)(2,1)S(1)}, u32[]{:S(2)}, u32[]{:S(2)}) collective-permute-start(bf16[2,64,128]{2,1,0:T(8,128)(2,1)S(1)} %get-tuple-element.10), channel_id=1, source_target_pairs={{0,32},{1,33},{2,34},{3,35},{4,36},{5,37},{6,38},{7,39},{8,40},{9,... | collective-permute-start | bytes 98312 | tf_op jit(solution)/shard_map/ppermute | solution.py:280
  6.7 14.3 %collective-permute-start.8 = (s16[8,128,128]{2,1,0:T(8,128)(2,1)S(1)}, s16[8,128,128]{2,1,0:T(8,128)(2,1)S(1)}, u32[]{:S(2)}, u32[]{:S(2)}) collective-permute-start(s16[8,128,128]{2,1,0:T(8,128)(2,1)S(1)} %get-tuple-element.12), channel_id=1, source_target_pairs={{0,1},{1,0},{2,3},{3,2},{4,5},{5,4},{6,7},{7,6},{8,9},{9,8},{10,11... | collective-permute-start | bytes 786440 | tf_op jit(solution)/shard_map/ppermute | solution.py:280
  7.9 9.6 %collective-permute-start.1 = (bf16[2,64,128]{2,1,0:T(8,128)(2,1)S(1)}, bf16[2,64,128]{2,1,0:T(8,128)(2,1)S(1)}, u32[]{:S(2)}, u32[]{:S(2)}) collective-permute-start(bf16[2,64,128]{2,1,0:T(8,128)(2,1)S(1)} %pad_maximum_fusion.2), channel_id=1, source_target_pairs={{0,64},{1,65},{2,66},{3,67},{4,68},{5,69},{6,70},{7,71},{8,72},{9,... | collective-permute-start | bytes 98312 | tf_op jit(solution)/shard_map/ppermute | solution.py:280
  17.5 5.5 %collective-permute-start.4 = (bf16[4,64,128]{2,1,0:T(8,128)(2,1)S(1)}, bf16[4,64,128]{2,1,0:T(8,128)(2,1)S(1)}, u32[]{:S(2)}, u32[]{:S(2)}) collective-permute-start(bf16[4,64,128]{2,1,0:T(8,128)(2,1)S(1)} %get-tuple-element.14), channel_id=1, source_target_pairs={{0,6},{1,7},{2,0},{3,1},{4,2},{5,3},{6,4},{7,5},{8,14},{9,15},{10,... | collective-permute-start | bytes 196616 | tf_op jit(solution)/shard_map/ppermute | solution.py:280
  18.4 4.9 %collective-permute-start.3 = (bf16[4,64,128]{2,1,0:T(8,128)(2,1)S(1)}, bf16[4,64,128]{2,1,0:T(8,128)(2,1)S(1)}, u32[]{:S(2)}, u32[]{:S(2)}) collective-permute-start(bf16[4,64,128]{2,1,0:T(8,128)(2,1)S(1)} %get-tuple-element.14), channel_id=1, source_target_pairs={{0,2},{1,3},{2,4},{3,5},{4,6},{5,7},{6,0},{7,1},{8,10},{9,11},{10,... | collective-permute-start | bytes 196616 | tf_op jit(solution)/shard_map/ppermute | solution.py:280
  20.8 5.8 %collective-permute-start.2 = (bf16[4,64,128]{2,1,0:T(8,128)(2,1)S(1)}, bf16[4,64,128]{2,1,0:T(8,128)(2,1)S(1)}, u32[]{:S(2)}, u32[]{:S(2)}) collective-permute-start(bf16[4,64,128]{2,1,0:T(8,128)(2,1)S(1)} %get-tuple-element.14), channel_id=1, source_target_pairs={{0,4},{1,5},{2,6},{3,7},{4,0},{5,1},{6,2},{7,3},{8,12},{9,13},{10,... | collective-permute-start | bytes 196616 | tf_op jit(solution)/shard_map/ppermute | solution.py:280
  21.0 12.1 %collective-permute-start.9 = (s16[8,128,128]{2,1,0:T(8,128)(2,1)S(1)}, s16[8,128,128]{2,1,0:T(8,128)(2,1)S(1)}, u32[]{:S(2)}, u32[]{:S(2)}) collective-permute-start(s16[8,128,128]{2,1,0:T(8,128)(2,1)S(1)} %collective-permute-done.8.refs_1_), channel_id=1, source_target_pairs={{0,32},{1,33},{2,34},{3,35},{4,36},{5,37},{6,38},{7,39},{8,40},{9,... | collective-permute-start | bytes 786440 | tf_op jit(solution)/shard_map/ppermute | solution.py:280
  26.6 11.4 %collective-permute-start.5 = (bf16[4,4,64,128]{3,2,1,0:T(8,128)(2,1)S(1)}, bf16[4,4,64,128]{3,2,1,0:T(8,128)(2,1)S(1)}, u32[]{:S(2)}, u32[]{:S(2)}) collective-permute-start(bf16[4,4,64,128]{3,2,1,0:T(8,128)(2,1)S(1)} %pad_maximum_fusion.refs_0_), channel_id=1, source_target_pairs={{0,16},{1,17},{2,18},{3,19},{4,20},{5,21},{6,22},{7,23},{8,24},{9,... | collective-permute-start | bytes 786440 | tf_op jit(solution)/shard_map/ppermute | solution.py:280
  29.9 8.2 %collective-permute-start.6 = (bf16[4,4,64,128]{3,2,1,0:T(8,128)(2,1)S(1)}, bf16[4,4,64,128]{3,2,1,0:T(8,128)(2,1)S(1)}, u32[]{:S(2)}, u32[]{:S(2)}) collective-permute-start(bf16[4,4,64,128]{3,2,1,0:T(8,128)(2,1)S(1)} %pad_maximum_fusion.refs_0_), channel_id=1, source_target_pairs={{0,8},{1,9},{2,10},{3,11},{4,12},{5,13},{6,14},{7,15},{8,16},{9,17... | collective-permute-start | bytes 786440 | tf_op jit(solution)/shard_map/ppermute | solution.py:280
  30.5 8.2 %collective-permute-start.7 = (bf16[4,4,64,128]{3,2,1,0:T(8,128)(2,1)S(1)}, bf16[4,4,64,128]{3,2,1,0:T(8,128)(2,1)S(1)}, u32[]{:S(2)}, u32[]{:S(2)}) collective-permute-start(bf16[4,4,64,128]{3,2,1,0:T(8,128)(2,1)S(1)} %pad_maximum_fusion.refs_0_), channel_id=1, source_target_pairs={{0,24},{1,25},{2,26},{3,27},{4,28},{5,29},{6,30},{7,31},{8,0},{9,1... | collective-permute-start | bytes 786440 | tf_op jit(solution)/shard_map/ppermute | solution.py:280
  39.2 9.2 %collective-permute-start.10 = (bf16[2,128,128]{2,1,0:T(8,128)(2,1)S(1)}, bf16[2,128,128]{2,1,0:T(8,128)(2,1)S(1)}, u32[]{:S(2)}, u32[]{:S(2)}) collective-permute-start(bf16[2,128,128]{2,1,0:T(8,128)(2,1)S(1)} %apply.7), channel_id=1, source_target_pairs={{0,1},{1,0},{2,3},{3,2},{4,5},{5,4},{6,7},{7,6},{8,9},{9,8},{10,11... | collective-permute-start | bytes 196616 | tf_op jit(solution)/shard_map/ppermute | solution.py:280

commit v2 on v1

--- a/solution.py
+++ b/solution.py
@@ -100,9 +100,7 @@
         mine[j] = jnp.where(zl == 0, first, second).astype(jnp.int16)
         other = jnp.where(zl == 0, second, first).astype(jnp.int16)
 
-        @pl.when(j // half.shape[0] == core)
-        def _():
-            half[j % half.shape[0]] = other
+        half[j] = other
 
     for b in range(n_bins):
         rows = jnp.concatenate([sums[:, b, :], sums[:, n_bins + b, :]], axis=0)
@@ -127,7 +125,7 @@
             pltpu.VMEM(block, jnp.bfloat16),
             pltpu.VMEM(block, jnp.bfloat16),
             pltpu.VMEM((blocks, points, 128), jnp.int16),
-            pltpu.VMEM((blocks // 2, points, 128), jnp.int16),
+            pltpu.VMEM((blocks, points, 128), jnp.int16),
         ],
         scratch_shapes=[
             pltpu.SMEM((n_bins,), jnp.int32),
@@ -284,7 +282,7 @@
     keep, give, own_delays, half = transform(bin_ids, delays, samples)
     got = send(give, lambda zh, c, y, x, zl: (zh, 1 - c, y, x, zl))
     half = send(half, lambda zh, c, y, x, zl: (zh, c, y, x, 1 - zl))
-    partner_delays = half, send(half, lambda zh, c, y, x, zl: (zh, 1 - c, y, x, zl))
+    partner_delays = (half,)
     away = jnp.concatenate([keep[1:], got[1:]])
     far = send(away, lambda zh, c, y, x, zl: (1 - zh, c, y, x, zl))
     column = jnp.concatenate([keep[:1], got[:1], far])
@@ -309,8 +307,8 @@
     for d in SHIFTS:
         planes.append(send(line, second(d)))
     theirs = apply_tables(planes[:1], (partner,), 0, None, None)
-    theirs = apply_tables(planes[1:3], (partner,), 2, theirs, None)
-    theirs = apply_tables(planes[3:], (partner,), 6, theirs, jnp.bfloat16)
+    theirs = apply_tables(planes[2:], (partner,), 4, theirs, None)
+    theirs = apply_tables(planes[1:2], (partner,), 2, theirs, jnp.bfloat16)
     theirs = send(theirs, lambda zh, c, y, x, zl: (zh, c, y, x, 1 - zl))
     mine = apply_tables(planes, own, 0, None, jnp.float32)
     seg_count = samples.shape[0] * lax.axis_size("tm")

time: 49.2 us -> 44.7 us (0.909)
  the two profiles are of different devices: /device:TPU:38 before, /device:TPU:6 now
where the time goes in v2:
time: 44.7 us; the launch traced here: 44.6 us
  Pallas kernels  20.1 us (45%)
  starting transfers between devices  15.9 us (36%)
  waiting for transfers between devices  8.34 us (19%)
    ppermute x10, starting transfers between devices, send(): return lax.ppermute(value, AXES, route(move))  15.9 us
    pallas_call x4, Pallas kernels, steer_tables(): pl.pallas_call(lambda *refs: steer_kernel(start, len(delays) == 2, *refs)...  10 us
    ppermute x10, waiting for transfers between devices, send(): return lax.ppermute(value, AXES, route(move))  8.34 us
    pallas_call x1, Pallas kernels, transform(): pl.pallas_call(transform_kernel, in_specs=[pl.BlockSpec(memory_space=pltp...  6.52 us
    pallas_call x4, Pallas kernels, apply_tables(): pl.pallas_call(lambda *refs: apply_kernel(len(planes), len(tables), start...  2.89 us
  transfers between devices with their start and end apart: 10, of which 5 were waited for; matrix products, arithmetic and copies ran while one was open for 0% of the time, Pallas kernels for 28%

profile of v2, /device:TPU:6, one launch (start us, length us, event | category | flops | bytes accessed | tf_op | source)
XLA Modules:
  0.0 44.6 jit_solution(4344517589614269862)
XLA Ops:
  0.0 0.0 copy-start
  0.0 6.5 %transform.1 = (bf16[2,64,128]{2,1,0:T(8,128)(2,1)S(1)}, bf16[2,64,128]{2,1,0:T(8,128)(2,1)S(1)}, s16[16,128,128]{2,1,0:T(8,128)(2,1)S(1)}, s16[16,128,128]{2,1,0:T(8,128)(2,1)S(1)}) custom-call(s32[16]{0:T(128)} %refs_0_.7, s32[128,4096]{1,0:T(8,128)} %delays_in.1, bf16[8,128,4096]{2,1,0:T(8,128)(2,1)} %samples.1), custom_call_target="tpu_custom_call" | custom-call | tf_op jit(solution)/shard_map/transform/pallas_call | solution.py:120
  6.5 0.1 collective-permute-start
  6.6 1.2 %collective-permute-done = bf16[2,64,128]{2,1,0:T(8,128)(2,1)S(1)} collective-permute-done((bf16[2,64,128]{2,1,0:T(8,128)(2,1)S(1)}, bf16[2,64,128]{2,1,0:T(8,128)(2,1)S(1)}, u32[]{:S(2)}, u32[]{:S(2)}) %collective-permute-start) | collective-permute-done | bytes 32800 | tf_op jit(solution)/shard_map/ppermute | solution.py:278
  7.8 4.0 %collective-permute-start.1 = (bf16[2,64,128]{2,1,0:T(8,128)(2,1)S(1)}, bf16[2,64,128]{2,1,0:T(8,128)(2,1)S(1)}, u32[]{:S(2)}, u32[]{:S(2)}) collective-permute-start(bf16[2,64,128]{2,1,0:T(8,128)(2,1)S(1)} %pad_maximum_fusion.2), channel_id=1, source_target_pairs={{0,64},{1,65},{2,66},{3,67},{4,68},{5,69},{6,70},{7,71},{8,72},{9,... | collective-permute-start | bytes 98312 | tf_op jit(solution)/shard_map/ppermute | solution.py:278
  11.8 1.0 %collective-permute-start.8 = (s16[16,128,128]{2,1,0:T(8,128)(2,1)S(1)}, s16[16,128,128]{2,1,0:T(8,128)(2,1)S(1)}, u32[]{:S(2)}, u32[]{:S(2)}) collective-permute-start(s16[16,128,128]{2,1,0:T(8,128)(2,1)S(1)} %get-tuple-element.12), channel_id=1, source_target_pairs={{0,1},{1,0},{2,3},{3,2},{4,5},{5,4},{6,7},{7,6},{8,9},{9,8},{10,11... | collective-permute-start | bytes 1572872 | tf_op jit(solution)/shard_map/ppermute | solution.py:278
  12.8 0.9 %collective-permute-done.1 = bf16[2,64,128]{2,1,0:T(8,128)(2,1)S(1)} collective-permute-done((bf16[2,64,128]{2,1,0:T(8,128)(2,1)S(1)}, bf16[2,64,128]{2,1,0:T(8,128)(2,1)S(1)}, u32[]{:S(2)}, u32[]{:S(2)}) %collective-permute-start.1) | collective-permute-done | bytes 32800 | tf_op jit(solution)/shard_map/ppermute | solution.py:278
  13.7 1.5 %collective-permute-start.2 = (bf16[4,64,128]{2,1,0:T(8,128)(2,1)S(1)}, bf16[4,64,128]{2,1,0:T(8,128)(2,1)S(1)}, u32[]{:S(2)}, u32[]{:S(2)}) collective-permute-start(bf16[4,64,128]{2,1,0:T(8,128)(2,1)S(1)} %get-tuple-element.14), channel_id=1, source_target_pairs={{0,4},{1,5},{2,6},{3,7},{4,0},{5,1},{6,2},{7,3},{8,12},{9,13},{10,... | collective-permute-start | bytes 196616 | tf_op jit(solution)/shard_map/ppermute | solution.py:278
  15.2 2.1 %collective-permute-start.3 = (bf16[4,64,128]{2,1,0:T(8,128)(2,1)S(1)}, bf16[4,64,128]{2,1,0:T(8,128)(2,1)S(1)}, u32[]{:S(2)}, u32[]{:S(2)}) collective-permute-start(bf16[4,64,128]{2,1,0:T(8,128)(2,1)S(1)} %get-tuple-element.14), channel_id=1, source_target_pairs={{0,2},{1,3},{2,4},{3,5},{4,6},{5,7},{6,0},{7,1},{8,10},{9,11},{10,... | collective-permute-start | bytes 196616 | tf_op jit(solution)/shard_map/ppermute | solution.py:278
  17.3 0.0 collective-permute-start.4
  17.3 2.3 %collective-permute-done.2 = bf16[4,64,128]{2,1,0:T(8,128)(2,1)S(1)} collective-permute-done((bf16[4,64,128]{2,1,0:T(8,128)(2,1)S(1)}, bf16[4,64,128]{2,1,0:T(8,128)(2,1)S(1)}, u32[]{:S(2)}, u32[]{:S(2)}) %collective-permute-start.2) | collective-permute-done | bytes 65568 | tf_op jit(solution)/shard_map/ppermute | solution.py:278
  19.5 0.0 collective-permute-done.3
  19.5 3.2 %collective-permute-done.4 = bf16[4,64,128]{2,1,0:T(8,128)(2,1)S(1)} collective-permute-done((bf16[4,64,128]{2,1,0:T(8,128)(2,1)S(1)}, bf16[4,64,128]{2,1,0:T(8,128)(2,1)S(1)}, u32[]{:S(2)}, u32[]{:S(2)}) %collective-permute-start.4) | collective-permute-done | bytes 65568 | tf_op jit(solution)/shard_map/ppermute | solution.py:278
  22.8 1.6 %collective-permute-start.6 = (bf16[4,4,64,128]{3,2,1,0:T(8,128)(2,1)S(1)}, bf16[4,4,64,128]{3,2,1,0:T(8,128)(2,1)S(1)}, u32[]{:S(2)}, u32[]{:S(2)}) collective-permute-start(bf16[4,4,64,128]{3,2,1,0:T(8,128)(2,1)S(1)} %pad_maximum_fusion.refs_0_), channel_id=1, source_target_pairs={{0,8},{1,9},{2,10},{3,11},{4,12},{5,13},{6,14},{7,15},{8,16},{9,17... | collective-permute-start | bytes 786440 | tf_op jit(solution)/shard_map/ppermute | solution.py:278
  24.4 1.7 %collective-permute-start.7 = (bf16[4,4,64,128]{3,2,1,0:T(8,128)(2,1)S(1)}, bf16[4,4,64,128]{3,2,1,0:T(8,128)(2,1)S(1)}, u32[]{:S(2)}, u32[]{:S(2)}) collective-permute-start(bf16[4,4,64,128]{3,2,1,0:T(8,128)(2,1)S(1)} %pad_maximum_fusion.refs_0_), channel_id=1, source_target_pairs={{0,24},{1,25},{2,26},{3,27},{4,28},{5,29},{6,30},{7,31},{8,0},{9,1... | collective-permute-start | bytes 786440 | tf_op jit(solution)/shard_map/ppermute | solution.py:278
  26.1 2.0 %collective-permute-start.5 = (bf16[4,4,64,128]{3,2,1,0:T(8,128)(2,1)S(1)}, bf16[4,4,64,128]{3,2,1,0:T(8,128)(2,1)S(1)}, u32[]{:S(2)}, u32[]{:S(2)}) collective-permute-start(bf16[4,4,64,128]{3,2,1,0:T(8,128)(2,1)S(1)} %pad_maximum_fusion.refs_0_), channel_id=1, source_target_pairs={{0,16},{1,17},{2,18},{3,19},{4,20},{5,21},{6,22},{7,23},{8,24},{9,... | collective-permute-start | bytes 786440 | tf_op jit(solution)/shard_map/ppermute | solution.py:278
  28.1 0.0 collective-permute-done.8.refs_1_
  28.1 0.0 copy-done
  28.1 4.4 %steer.7.refs_1_.refs_2_ = bf16[8,4,128,512]{3,2,1,0:T(8,128)(2,1)S(1)} custom-call(s32[16]{0:T(128)S(1)} %copy-done, s16[16,128,128]{2,1,0:T(8,128)(2,1)S(1)} %collective-permute-done.8.refs_1_), custom_call_target="tpu_custom_call" | custom-call | tf_op jit(solution)/shard_map/steer/pallas_call | solution.py:185
  32.5 0.4 apply.5.refs_3_
  33.0 0.0 collective-permute-done.6.refs_2_.refs_0_
  33.0 0.0 collective-permute-done.7.refs_3_.refs_1_
  33.0 0.7 %apply.6.refs_2_ = f32[4,128,64]{2,1,0:T(8,128)S(1)} custom-call(bf16[4,4,64,128]{3,2,1,0:T(8,128)(2,1)S(1)} %collective-permute-done.6.refs_2_.refs_0_, bf16[4,4,64,128]{3,2,1,0:T(8,128)(2,1)S(1)} %collective-permute-done.7.refs_3_.refs_1_, bf16[8,4,128,512]{3,2,1,0:T(8,128)(2,1)S(1)} %steer.7.refs_1_.refs_2_, f32[4,128,64]{2,1,0:T(8,128)S(1)} %apply.5.refs_3_), custom_call_target="tpu_custom_call" | custom-call | tf_op jit(solution)/shard_map/apply/pallas_call | solution.py:235
  33.7 0.8 %collective-permute-done.5.refs_1_.refs_0_ = bf16[4,4,64,128]{3,2,1,0:T(8,128)(2,1)S(1)} collective-permute-done((bf16[4,4,64,128]{3,2,1,0:T(8,128)(2,1)S(1)}, bf16[4,4,64,128]{3,2,1,0:T(8,128)(2,1)S(1)}, u32[]{:S(2)}, u32[]{:S(2)}) %collective-permute-start.5) | collective-permute-done | bytes 262176 | tf_op jit(solution)/shard_map/ppermute | solution.py:278
  34.5 0.5 %apply.7 = bf16[2,128,128]{2,1,0:T(8,128)(2,1)S(1)} custom-call(bf16[4,4,64,128]{3,2,1,0:T(8,128)(2,1)S(1)} %collective-permute-done.5.refs_1_.refs_0_, bf16[8,4,128,512]{3,2,1,0:T(8,128)(2,1)S(1)} %steer.7.refs_1_.refs_2_, f32[4,128,64]{2,1,0:T(8,128)S(1)} %apply.6.refs_2_), custom_call_target="tpu_custom_call" | custom-call | tf_op jit(solution)/shard_map/apply/pallas_call | solution.py:235
  35.0 2.0 %collective-permute-start.9 = (bf16[2,128,128]{2,1,0:T(8,128)(2,1)S(1)}, bf16[2,128,128]{2,1,0:T(8,128)(2,1)S(1)}, u32[]{:S(2)}, u32[]{:S(2)}) collective-permute-start(bf16[2,128,128]{2,1,0:T(8,128)(2,1)S(1)} %apply.7), channel_id=1, source_target_pairs={{0,1},{1,0},{2,3},{3,2},{4,5},{5,4},{6,7},{7,6},{8,9},{9,8},{10,11... | collective-permute-start | bytes 196616 | tf_op jit(solution)/shard_map/ppermute | solution.py:278
  37.0 2.5 %steer.5.refs_5_ = bf16[4,4,128,512]{3,2,1,0:T(8,128)(2,1)S(1)} custom-call(s32[16]{0:T(128)S(1)} %copy-done, s16[16,128,128]{2,1,0:T(8,128)(2,1)S(1)} %get-tuple-element.11.refs_1_), custom_call_target="tpu_custom_call" | custom-call | tf_op jit(solution)/shard_map/steer/pallas_call | solution.py:185
  39.5 1.5 %steer.4.refs_4_ = bf16[2,4,128,512]{3,2,1,0:T(8,128)(2,1)S(1)} custom-call(s32[16]{0:T(128)S(1)} %copy-done, s16[16,128,128]{2,1,0:T(8,128)(2,1)S(1)} %get-tuple-element.11.refs_1_), custom_call_target="tpu_custom_call" | custom-call | tf_op jit(solution)/shard_map/steer/pallas_call | solution.py:185
  41.0 1.5 %steer.6.refs_6_ = bf16[2,4,128,512]{3,2,1,0:T(8,128)(2,1)S(1)} custom-call(s32[16]{0:T(128)S(1)} %copy-done, s16[16,128,128]{2,1,0:T(8,128)(2,1)S(1)} %get-tuple-element.11.refs_1_), custom_call_target="tpu_custom_call" | custom-call | tf_op jit(solution)/shard_map/steer/pallas_call | solution.py:185
  42.6 1.3 %apply.4.refs_0_ = f32[2,128,128]{2,1,0:T(8,128)S(1)} custom-call(bf16[4,4,64,128]{3,2,1,0:T(8,128)(2,1)S(1)} %pad_maximum_fusion.refs_0_, bf16[4,4,64,128]{3,2,1,0:T(8,128)(2,1)S(1)} %collective-permute-done.5.refs_1_.refs_0_, bf16[4,4,64,128]{3,2,1,0:T(8,128)(2,1)S(1)} %collective-permute-done.6.refs_2_.refs_0_, ...), custom_call_target="tpu_custom_call" | custom-call | tf_op jit(solution)/shard_map/apply/pallas_call | solution.py:235
  43.9 0.0 collective-permute-done.9.refs_1_
  43.9 0.7 %powers.1 = f32[4,128]{1,0:T(4,128)} custom-call(f32[2,128,128]{2,1,0:T(8,128)S(1)} %apply.4.refs_0_, bf16[2,128,128]{2,1,0:T(8,128)(2,1)S(1)} %collective-permute-done.9.refs_1_), custom_call_target="tpu_custom_call" | custom-call | tf_op jit(solution)/shard_map/powers/pallas_call | solution.py:257
  (5 shorter events, 0.1 us)
Async XLA Ops:
  0.0 28.1 %copy-start = (s32[16]{0:T(128)S(1)}, s32[16]{0:T(128)}, u32[]{:S(2)}) copy-start(s32[16]{0:T(128)} %refs_0_.7) | copy-start | bytes 196
  6.5 1.3 %collective-permute-start = (bf16[2,64,128]{2,1,0:T(8,128)(2,1)S(1)}, bf16[2,64,128]{2,1,0:T(8,128)(2,1)S(1)}, u32[]{:S(2)}, u32[]{:S(2)}) collective-permute-start(bf16[2,64,128]{2,1,0:T(8,128)(2,1)S(1)} %get-tuple-element.10), channel_id=1, source_target_pairs={{0,32},{1,33},{2,34},{3,35},{4,36},{5,37},{6,38},{7,39},{8,40},{9,... | collective-permute-start | bytes 98312 | tf_op jit(solution)/shard_map/ppermute | solution.py:278
  7.8 5.9 %collective-permute-start.1 = (bf16[2,64,128]{2,1,0:T(8,128)(2,1)S(1)}, bf16[2,64,128]{2,1,0:T(8,128)(2,1)S(1)}, u32[]{:S(2)}, u32[]{:S(2)}) collective-permute-start(bf16[2,64,128]{2,1,0:T(8,128)(2,1)S(1)} %pad_maximum_fusion.2), channel_id=1, source_target_pairs={{0,64},{1,65},{2,66},{3,67},{4,68},{5,69},{6,70},{7,71},{8,72},{9,... | collective-permute-start | bytes 98312 | tf_op jit(solution)/shard_map/ppermute | solution.py:278
  11.8 16.3 %collective-permute-start.8 = (s16[16,128,128]{2,1,0:T(8,128)(2,1)S(1)}, s16[16,128,128]{2,1,0:T(8,128)(2,1)S(1)}, u32[]{:S(2)}, u32[]{:S(2)}) collective-permute-start(s16[16,128,128]{2,1,0:T(8,128)(2,1)S(1)} %get-tuple-element.12), channel_id=1, source_target_pairs={{0,1},{1,0},{2,3},{3,2},{4,5},{5,4},{6,7},{7,6},{8,9},{9,8},{10,11... | collective-permute-start | bytes 1572872 | tf_op jit(solution)/shard_map/ppermute | solution.py:278
  13.7 5.8 %collective-permute-start.2 = (bf16[4,64,128]{2,1,0:T(8,128)(2,1)S(1)}, bf16[4,64,128]{2,1,0:T(8,128)(2,1)S(1)}, u32[]{:S(2)}, u32[]{:S(2)}) collective-permute-start(bf16[4,64,128]{2,1,0:T(8,128)(2,1)S(1)} %get-tuple-element.14), channel_id=1, source_target_pairs={{0,4},{1,5},{2,6},{3,7},{4,0},{5,1},{6,2},{7,3},{8,12},{9,13},{10,... | collective-permute-start | bytes 196616 | tf_op jit(solution)/shard_map/ppermute | solution.py:278
  15.2 4.4 %collective-permute-start.3 = (bf16[4,64,128]{2,1,0:T(8,128)(2,1)S(1)}, bf16[4,64,128]{2,1,0:T(8,128)(2,1)S(1)}, u32[]{:S(2)}, u32[]{:S(2)}) collective-permute-start(bf16[4,64,128]{2,1,0:T(8,128)(2,1)S(1)} %get-tuple-element.14), channel_id=1, source_target_pairs={{0,2},{1,3},{2,4},{3,5},{4,6},{5,7},{6,0},{7,1},{8,10},{9,11},{10,... | collective-permute-start | bytes 196616 | tf_op jit(solution)/shard_map/ppermute | solution.py:278
  17.3 5.5 %collective-permute-start.4 = (bf16[4,64,128]{2,1,0:T(8,128)(2,1)S(1)}, bf16[4,64,128]{2,1,0:T(8,128)(2,1)S(1)}, u32[]{:S(2)}, u32[]{:S(2)}) collective-permute-start(bf16[4,64,128]{2,1,0:T(8,128)(2,1)S(1)} %get-tuple-element.14), channel_id=1, source_target_pairs={{0,6},{1,7},{2,0},{3,1},{4,2},{5,3},{6,4},{7,5},{8,14},{9,15},{10,... | collective-permute-start | bytes 196616 | tf_op jit(solution)/shard_map/ppermute | solution.py:278
  22.8 10.2 %collective-permute-start.6 = (bf16[4,4,64,128]{3,2,1,0:T(8,128)(2,1)S(1)}, bf16[4,4,64,128]{3,2,1,0:T(8,128)(2,1)S(1)}, u32[]{:S(2)}, u32[]{:S(2)}) collective-permute-start(bf16[4,4,64,128]{3,2,1,0:T(8,128)(2,1)S(1)} %pad_maximum_fusion.refs_0_), channel_id=1, source_target_pairs={{0,8},{1,9},{2,10},{3,11},{4,12},{5,13},{6,14},{7,15},{8,16},{9,17... | collective-permute-start | bytes 786440 | tf_op jit(solution)/shard_map/ppermute | solution.py:278
  24.4 8.5 %collective-permute-start.7 = (bf16[4,4,64,128]{3,2,1,0:T(8,128)(2,1)S(1)}, bf16[4,4,64,128]{3,2,1,0:T(8,128)(2,1)S(1)}, u32[]{:S(2)}, u32[]{:S(2)}) collective-permute-start(bf16[4,4,64,128]{3,2,1,0:T(8,128)(2,1)S(1)} %pad_maximum_fusion.refs_0_), channel_id=1, source_target_pairs={{0,24},{1,25},{2,26},{3,27},{4,28},{5,29},{6,30},{7,31},{8,0},{9,1... | collective-permute-start | bytes 786440 | tf_op jit(solution)/shard_map/ppermute | solution.py:278
  26.1 8.4 %collective-permute-start.5 = (bf16[4,4,64,128]{3,2,1,0:T(8,128)(2,1)S(1)}, bf16[4,4,64,128]{3,2,1,0:T(8,128)(2,1)S(1)}, u32[]{:S(2)}, u32[]{:S(2)}) collective-permute-start(bf16[4,4,64,128]{3,2,1,0:T(8,128)(2,1)S(1)} %pad_maximum_fusion.refs_0_), channel_id=1, source_target_pairs={{0,16},{1,17},{2,18},{3,19},{4,20},{5,21},{6,22},{7,23},{8,24},{9,... | collective-permute-start | bytes 786440 | tf_op jit(solution)/shard_map/ppermute | solution.py:278
  35.0 8.9 %collective-permute-start.9 = (bf16[2,128,128]{2,1,0:T(8,128)(2,1)S(1)}, bf16[2,128,128]{2,1,0:T(8,128)(2,1)S(1)}, u32[]{:S(2)}, u32[]{:S(2)}) collective-permute-start(bf16[2,128,128]{2,1,0:T(8,128)(2,1)S(1)} %apply.7), channel_id=1, source_target_pairs={{0,1},{1,0},{2,3},{3,2},{4,5},{5,4},{6,7},{7,6},{8,9},{9,8},{10,11... | collective-permute-start | bytes 196616 | tf_op jit(solution)/shard_map/ppermute | solution.py:278

commit v3 on v2

--- a/solution.py
+++ b/solution.py
@@ -11,7 +11,8 @@
 AXES = ("tm", "mic")
 SHIFTS = (2, 1, 3)
 ROUND = 12582912.0
-GROUPS = (3, 3, 2)
+GROUPS = (2, 3, 3)
+AHEAD = 4
 OWN = (2, 4, 2)
 SIN_POLY = (4.442882919124343, -7.30824568650904, 3.6063542184324877, -0.8461116503718901, 0.10982451642219883)
 COS_POLY = (1.414213496255228, -6.978850948563807, 5.73946037690717, -1.8835579059870113, 0.31068802752761115)
@@ -57,7 +58,7 @@
     bins_copy = pltpu.make_async_copy(bins_in, bins, sems.at[n_segs])
     delays_copy = pltpu.make_async_copy(delays_in, delays, sems.at[n_segs + 1])
     bins_copy.start()
-    for s in range(GROUPS[0]):
+    for s in range(AHEAD):
         copies[s].start()
 
     bins_copy.wait()
@@ -78,8 +79,8 @@
     for g, group in enumerate(GROUPS):
         for s in range(done, done + group):
             copies[s].wait()
-            if s + GROUPS[0] < n_segs:
-                copies[s + GROUPS[0]].start()
+            if s + AHEAD < n_segs:
+                copies[s + AHEAD].start()
         if g == 0:
             delays_copy.start()
         if g == len(GROUPS) - 1:

time: 44.7 us -> 44.3 us (level)
  no operation moved by 1% of the time
where the time goes in v3:
time: 44.3 us; the launch traced here: 44.2 us
  Pallas kernels  19.7 us (44%)
  starting transfers between devices  15.9 us (36%)
  waiting for transfers between devices  8.35 us (19%)
    ppermute x10, starting transfers between devices, send(): return lax.ppermute(value, AXES, route(move))  15.9 us
    pallas_call x4, Pallas kernels, steer_tables(): pl.pallas_call(lambda *refs: steer_kernel(start, len(delays) == 2, *refs)...  10 us
    ppermute x10, waiting for transfers between devices, send(): return lax.ppermute(value, AXES, route(move))  8.35 us
    pallas_call x1, Pallas kernels, transform(): pl.pallas_call(transform_kernel, in_specs=[pl.BlockSpec(memory_space=pltp...  6.11 us
    pallas_call x4, Pallas kernels, apply_tables(): pl.pallas_call(lambda *refs: apply_kernel(len(planes), len(tables), start...  2.89 us
  transfers between devices with their start and end apart: 10, of which 5 were waited for; matrix products, arithmetic and copies ran while one was open for 0% of the time, Pallas kernels for 28%

profile of v3, /device:TPU:6, one launch (start us, length us, event | category | flops | bytes accessed | tf_op | source)
XLA Modules:
  0.0 44.2 jit_solution(9445899237396509940)
XLA Ops:
  0.0 0.0 copy-start
  0.0 6.1 %transform.1 = (bf16[2,64,128]{2,1,0:T(8,128)(2,1)S(1)}, bf16[2,64,128]{2,1,0:T(8,128)(2,1)S(1)}, s16[16,128,128]{2,1,0:T(8,128)(2,1)S(1)}, s16[16,128,128]{2,1,0:T(8,128)(2,1)S(1)}) custom-call(s32[16]{0:T(128)} %refs_0_.7, s32[128,4096]{1,0:T(8,128)} %delays_in.1, bf16[8,128,4096]{2,1,0:T(8,128)(2,1)} %samples.1), custom_call_target="tpu_custom_call" | custom-call | tf_op jit(solution)/shard_map/transform/pallas_call | solution.py:121
  6.1 0.1 collective-permute-start
  6.2 1.2 %collective-permute-done = bf16[2,64,128]{2,1,0:T(8,128)(2,1)S(1)} collective-permute-done((bf16[2,64,128]{2,1,0:T(8,128)(2,1)S(1)}, bf16[2,64,128]{2,1,0:T(8,128)(2,1)S(1)}, u32[]{:S(2)}, u32[]{:S(2)}) %collective-permute-start) | collective-permute-done | bytes 32800 | tf_op jit(solution)/shard_map/ppermute | solution.py:279
  7.4 4.0 %collective-permute-start.1 = (bf16[2,64,128]{2,1,0:T(8,128)(2,1)S(1)}, bf16[2,64,128]{2,1,0:T(8,128)(2,1)S(1)}, u32[]{:S(2)}, u32[]{:S(2)}) collective-permute-start(bf16[2,64,128]{2,1,0:T(8,128)(2,1)S(1)} %pad_maximum_fusion.2), channel_id=1, source_target_pairs={{0,64},{1,65},{2,66},{3,67},{4,68},{5,69},{6,70},{7,71},{8,72},{9,... | collective-permute-start | bytes 98312 | tf_op jit(solution)/shard_map/ppermute | solution.py:279
  11.4 1.0 %collective-permute-start.8 = (s16[16,128,128]{2,1,0:T(8,128)(2,1)S(1)}, s16[16,128,128]{2,1,0:T(8,128)(2,1)S(1)}, u32[]{:S(2)}, u32[]{:S(2)}) collective-permute-start(s16[16,128,128]{2,1,0:T(8,128)(2,1)S(1)} %get-tuple-element.12), channel_id=1, source_target_pairs={{0,1},{1,0},{2,3},{3,2},{4,5},{5,4},{6,7},{7,6},{8,9},{9,8},{10,11... | collective-permute-start | bytes 1572872 | tf_op jit(solution)/shard_map/ppermute | solution.py:279
  12.4 0.9 %collective-permute-done.1 = bf16[2,64,128]{2,1,0:T(8,128)(2,1)S(1)} collective-permute-done((bf16[2,64,128]{2,1,0:T(8,128)(2,1)S(1)}, bf16[2,64,128]{2,1,0:T(8,128)(2,1)S(1)}, u32[]{:S(2)}, u32[]{:S(2)}) %collective-permute-start.1) | collective-permute-done | bytes 32800 | tf_op jit(solution)/shard_map/ppermute | solution.py:279
  13.3 1.5 %collective-permute-start.2 = (bf16[4,64,128]{2,1,0:T(8,128)(2,1)S(1)}, bf16[4,64,128]{2,1,0:T(8,128)(2,1)S(1)}, u32[]{:S(2)}, u32[]{:S(2)}) collective-permute-start(bf16[4,64,128]{2,1,0:T(8,128)(2,1)S(1)} %get-tuple-element.14), channel_id=1, source_target_pairs={{0,4},{1,5},{2,6},{3,7},{4,0},{5,1},{6,2},{7,3},{8,12},{9,13},{10,... | collective-permute-start | bytes 196616 | tf_op jit(solution)/shard_map/ppermute | solution.py:279
  14.8 2.1 %collective-permute-start.3 = (bf16[4,64,128]{2,1,0:T(8,128)(2,1)S(1)}, bf16[4,64,128]{2,1,0:T(8,128)(2,1)S(1)}, u32[]{:S(2)}, u32[]{:S(2)}) collective-permute-start(bf16[4,64,128]{2,1,0:T(8,128)(2,1)S(1)} %get-tuple-element.14), channel_id=1, source_target_pairs={{0,2},{1,3},{2,4},{3,5},{4,6},{5,7},{6,0},{7,1},{8,10},{9,11},{10,... | collective-permute-start | bytes 196616 | tf_op jit(solution)/shard_map/ppermute | solution.py:279
  16.9 0.0 collective-permute-start.4
  16.9 2.3 %collective-permute-done.2 = bf16[4,64,128]{2,1,0:T(8,128)(2,1)S(1)} collective-permute-done((bf16[4,64,128]{2,1,0:T(8,128)(2,1)S(1)}, bf16[4,64,128]{2,1,0:T(8,128)(2,1)S(1)}, u32[]{:S(2)}, u32[]{:S(2)}) %collective-permute-start.2) | collective-permute-done | bytes 65568 | tf_op jit(solution)/shard_map/ppermute | solution.py:279
  19.1 0.0 collective-permute-done.3
  19.1 3.2 %collective-permute-done.4 = bf16[4,64,128]{2,1,0:T(8,128)(2,1)S(1)} collective-permute-done((bf16[4,64,128]{2,1,0:T(8,128)(2,1)S(1)}, bf16[4,64,128]{2,1,0:T(8,128)(2,1)S(1)}, u32[]{:S(2)}, u32[]{:S(2)}) %collective-permute-start.4) | collective-permute-done | bytes 65568 | tf_op jit(solution)/shard_map/ppermute | solution.py:279
  22.4 1.6 %collective-permute-start.6 = (bf16[4,4,64,128]{3,2,1,0:T(8,128)(2,1)S(1)}, bf16[4,4,64,128]{3,2,1,0:T(8,128)(2,1)S(1)}, u32[]{:S(2)}, u32[]{:S(2)}) collective-permute-start(bf16[4,4,64,128]{3,2,1,0:T(8,128)(2,1)S(1)} %pad_maximum_fusion.refs_0_), channel_id=1, source_target_pairs={{0,8},{1,9},{2,10},{3,11},{4,12},{5,13},{6,14},{7,15},{8,16},{9,17... | collective-permute-start | bytes 786440 | tf_op jit(solution)/shard_map/ppermute | solution.py:279
  24.0 1.7 %collective-permute-start.7 = (bf16[4,4,64,128]{3,2,1,0:T(8,128)(2,1)S(1)}, bf16[4,4,64,128]{3,2,1,0:T(8,128)(2,1)S(1)}, u32[]{:S(2)}, u32[]{:S(2)}) collective-permute-start(bf16[4,4,64,128]{3,2,1,0:T(8,128)(2,1)S(1)} %pad_maximum_fusion.refs_0_), channel_id=1, source_target_pairs={{0,24},{1,25},{2,26},{3,27},{4,28},{5,29},{6,30},{7,31},{8,0},{9,1... | collective-permute-start | bytes 786440 | tf_op jit(solution)/shard_map/ppermute | solution.py:279
  25.7 2.0 %collective-permute-start.5 = (bf16[4,4,64,128]{3,2,1,0:T(8,128)(2,1)S(1)}, bf16[4,4,64,128]{3,2,1,0:T(8,128)(2,1)S(1)}, u32[]{:S(2)}, u32[]{:S(2)}) collective-permute-start(bf16[4,4,64,128]{3,2,1,0:T(8,128)(2,1)S(1)} %pad_maximum_fusion.refs_0_), channel_id=1, source_target_pairs={{0,16},{1,17},{2,18},{3,19},{4,20},{5,21},{6,22},{7,23},{8,24},{9,... | collective-permute-start | bytes 786440 | tf_op jit(solution)/shard_map/ppermute | solution.py:279
  27.7 0.0 collective-permute-done.8.refs_1_
  27.7 0.0 copy-done
  27.7 4.4 %steer.7.refs_1_.refs_2_ = bf16[8,4,128,512]{3,2,1,0:T(8,128)(2,1)S(1)} custom-call(s32[16]{0:T(128)S(1)} %copy-done, s16[16,128,128]{2,1,0:T(8,128)(2,1)S(1)} %collective-permute-done.8.refs_1_), custom_call_target="tpu_custom_call" | custom-call | tf_op jit(solution)/shard_map/steer/pallas_call | solution.py:186
  32.1 0.4 apply.5.refs_3_
  32.6 0.0 collective-permute-done.6.refs_2_.refs_0_
  32.6 0.0 collective-permute-done.7.refs_3_.refs_1_
  32.6 0.7 %apply.6.refs_2_ = f32[4,128,64]{2,1,0:T(8,128)S(1)} custom-call(bf16[4,4,64,128]{3,2,1,0:T(8,128)(2,1)S(1)} %collective-permute-done.6.refs_2_.refs_0_, bf16[4,4,64,128]{3,2,1,0:T(8,128)(2,1)S(1)} %collective-permute-done.7.refs_3_.refs_1_, bf16[8,4,128,512]{3,2,1,0:T(8,128)(2,1)S(1)} %steer.7.refs_1_.refs_2_, f32[4,128,64]{2,1,0:T(8,128)S(1)} %apply.5.refs_3_), custom_call_target="tpu_custom_call" | custom-call | tf_op jit(solution)/shard_map/apply/pallas_call | solution.py:236
  33.3 0.8 %collective-permute-done.5.refs_1_.refs_0_ = bf16[4,4,64,128]{3,2,1,0:T(8,128)(2,1)S(1)} collective-permute-done((bf16[4,4,64,128]{3,2,1,0:T(8,128)(2,1)S(1)}, bf16[4,4,64,128]{3,2,1,0:T(8,128)(2,1)S(1)}, u32[]{:S(2)}, u32[]{:S(2)}) %collective-permute-start.5) | collective-permute-done | bytes 262176 | tf_op jit(solution)/shard_map/ppermute | solution.py:279
  34.1 0.5 %apply.7 = bf16[2,128,128]{2,1,0:T(8,128)(2,1)S(1)} custom-call(bf16[4,4,64,128]{3,2,1,0:T(8,128)(2,1)S(1)} %collective-permute-done.5.refs_1_.refs_0_, bf16[8,4,128,512]{3,2,1,0:T(8,128)(2,1)S(1)} %steer.7.refs_1_.refs_2_, f32[4,128,64]{2,1,0:T(8,128)S(1)} %apply.6.refs_2_), custom_call_target="tpu_custom_call" | custom-call | tf_op jit(solution)/shard_map/apply/pallas_call | solution.py:236
  34.6 2.0 %collective-permute-start.9 = (bf16[2,128,128]{2,1,0:T(8,128)(2,1)S(1)}, bf16[2,128,128]{2,1,0:T(8,128)(2,1)S(1)}, u32[]{:S(2)}, u32[]{:S(2)}) collective-permute-start(bf16[2,128,128]{2,1,0:T(8,128)(2,1)S(1)} %apply.7), channel_id=1, source_target_pairs={{0,1},{1,0},{2,3},{3,2},{4,5},{5,4},{6,7},{7,6},{8,9},{9,8},{10,11... | collective-permute-start | bytes 196616 | tf_op jit(solution)/shard_map/ppermute | solution.py:279
  36.6 2.5 %steer.5.refs_5_ = bf16[4,4,128,512]{3,2,1,0:T(8,128)(2,1)S(1)} custom-call(s32[16]{0:T(128)S(1)} %copy-done, s16[16,128,128]{2,1,0:T(8,128)(2,1)S(1)} %get-tuple-element.11.refs_1_), custom_call_target="tpu_custom_call" | custom-call | tf_op jit(solution)/shard_map/steer/pallas_call | solution.py:186
  39.1 1.5 %steer.4.refs_4_ = bf16[2,4,128,512]{3,2,1,0:T(8,128)(2,1)S(1)} custom-call(s32[16]{0:T(128)S(1)} %copy-done, s16[16,128,128]{2,1,0:T(8,128)(2,1)S(1)} %get-tuple-element.11.refs_1_), custom_call_target="tpu_custom_call" | custom-call | tf_op jit(solution)/shard_map/steer/pallas_call | solution.py:186
  40.6 1.5 %steer.6.refs_6_ = bf16[2,4,128,512]{3,2,1,0:T(8,128)(2,1)S(1)} custom-call(s32[16]{0:T(128)S(1)} %copy-done, s16[16,128,128]{2,1,0:T(8,128)(2,1)S(1)} %get-tuple-element.11.refs_1_), custom_call_target="tpu_custom_call" | custom-call | tf_op jit(solution)/shard_map/steer/pallas_call | solution.py:186
  42.2 1.3 %apply.4.refs_0_ = f32[2,128,128]{2,1,0:T(8,128)S(1)} custom-call(bf16[4,4,64,128]{3,2,1,0:T(8,128)(2,1)S(1)} %pad_maximum_fusion.refs_0_, bf16[4,4,64,128]{3,2,1,0:T(8,128)(2,1)S(1)} %collective-permute-done.5.refs_1_.refs_0_, bf16[4,4,64,128]{3,2,1,0:T(8,128)(2,1)S(1)} %collective-permute-done.6.refs_2_.refs_0_, ...), custom_call_target="tpu_custom_call" | custom-call | tf_op jit(solution)/shard_map/apply/pallas_call | solution.py:236
  43.5 0.0 collective-permute-done.9.refs_1_
  43.5 0.7 %powers.1 = f32[4,128]{1,0:T(4,128)} custom-call(f32[2,128,128]{2,1,0:T(8,128)S(1)} %apply.4.refs_0_, bf16[2,128,128]{2,1,0:T(8,128)(2,1)S(1)} %collective-permute-done.9.refs_1_), custom_call_target="tpu_custom_call" | custom-call | tf_op jit(solution)/shard_map/powers/pallas_call | solution.py:258
  (5 shorter events, 0.1 us)
Async XLA Ops:
  0.0 27.7 %copy-start = (s32[16]{0:T(128)S(1)}, s32[16]{0:T(128)}, u32[]{:S(2)}) copy-start(s32[16]{0:T(128)} %refs_0_.7) | copy-start | bytes 196
  6.1 1.3 %collective-permute-start = (bf16[2,64,128]{2,1,0:T(8,128)(2,1)S(1)}, bf16[2,64,128]{2,1,0:T(8,128)(2,1)S(1)}, u32[]{:S(2)}, u32[]{:S(2)}) collective-permute-start(bf16[2,64,128]{2,1,0:T(8,128)(2,1)S(1)} %get-tuple-element.10), channel_id=1, source_target_pairs={{0,32},{1,33},{2,34},{3,35},{4,36},{5,37},{6,38},{7,39},{8,40},{9,... | collective-permute-start | bytes 98312 | tf_op jit(solution)/shard_map/ppermute | solution.py:279
  7.4 5.9 %collective-permute-start.1 = (bf16[2,64,128]{2,1,0:T(8,128)(2,1)S(1)}, bf16[2,64,128]{2,1,0:T(8,128)(2,1)S(1)}, u32[]{:S(2)}, u32[]{:S(2)}) collective-permute-start(bf16[2,64,128]{2,1,0:T(8,128)(2,1)S(1)} %pad_maximum_fusion.2), channel_id=1, source_target_pairs={{0,64},{1,65},{2,66},{3,67},{4,68},{5,69},{6,70},{7,71},{8,72},{9,... | collective-permute-start | bytes 98312 | tf_op jit(solution)/shard_map/ppermute | solution.py:279
  11.4 16.3 %collective-permute-start.8 = (s16[16,128,128]{2,1,0:T(8,128)(2,1)S(1)}, s16[16,128,128]{2,1,0:T(8,128)(2,1)S(1)}, u32[]{:S(2)}, u32[]{:S(2)}) collective-permute-start(s16[16,128,128]{2,1,0:T(8,128)(2,1)S(1)} %get-tuple-element.12), channel_id=1, source_target_pairs={{0,1},{1,0},{2,3},{3,2},{4,5},{5,4},{6,7},{7,6},{8,9},{9,8},{10,11... | collective-permute-start | bytes 1572872 | tf_op jit(solution)/shard_map/ppermute | solution.py:279
  13.3 5.8 %collective-permute-start.2 = (bf16[4,64,128]{2,1,0:T(8,128)(2,1)S(1)}, bf16[4,64,128]{2,1,0:T(8,128)(2,1)S(1)}, u32[]{:S(2)}, u32[]{:S(2)}) collective-permute-start(bf16[4,64,128]{2,1,0:T(8,128)(2,1)S(1)} %get-tuple-element.14), channel_id=1, source_target_pairs={{0,4},{1,5},{2,6},{3,7},{4,0},{5,1},{6,2},{7,3},{8,12},{9,13},{10,... | collective-permute-start | bytes 196616 | tf_op jit(solution)/shard_map/ppermute | solution.py:279
  14.8 4.4 %collective-permute-start.3 = (bf16[4,64,128]{2,1,0:T(8,128)(2,1)S(1)}, bf16[4,64,128]{2,1,0:T(8,128)(2,1)S(1)}, u32[]{:S(2)}, u32[]{:S(2)}) collective-permute-start(bf16[4,64,128]{2,1,0:T(8,128)(2,1)S(1)} %get-tuple-element.14), channel_id=1, source_target_pairs={{0,2},{1,3},{2,4},{3,5},{4,6},{5,7},{6,0},{7,1},{8,10},{9,11},{10,... | collective-permute-start | bytes 196616 | tf_op jit(solution)/shard_map/ppermute | solution.py:279
  16.9 5.5 %collective-permute-start.4 = (bf16[4,64,128]{2,1,0:T(8,128)(2,1)S(1)}, bf16[4,64,128]{2,1,0:T(8,128)(2,1)S(1)}, u32[]{:S(2)}, u32[]{:S(2)}) collective-permute-start(bf16[4,64,128]{2,1,0:T(8,128)(2,1)S(1)} %get-tuple-element.14), channel_id=1, source_target_pairs={{0,6},{1,7},{2,0},{3,1},{4,2},{5,3},{6,4},{7,5},{8,14},{9,15},{10,... | collective-permute-start | bytes 196616 | tf_op jit(solution)/shard_map/ppermute | solution.py:279
  22.4 10.2 %collective-permute-start.6 = (bf16[4,4,64,128]{3,2,1,0:T(8,128)(2,1)S(1)}, bf16[4,4,64,128]{3,2,1,0:T(8,128)(2,1)S(1)}, u32[]{:S(2)}, u32[]{:S(2)}) collective-permute-start(bf16[4,4,64,128]{3,2,1,0:T(8,128)(2,1)S(1)} %pad_maximum_fusion.refs_0_), channel_id=1, source_target_pairs={{0,8},{1,9},{2,10},{3,11},{4,12},{5,13},{6,14},{7,15},{8,16},{9,17... | collective-permute-start | bytes 786440 | tf_op jit(solution)/shard_map/ppermute | solution.py:279
  24.0 8.5 %collective-permute-start.7 = (bf16[4,4,64,128]{3,2,1,0:T(8,128)(2,1)S(1)}, bf16[4,4,64,128]{3,2,1,0:T(8,128)(2,1)S(1)}, u32[]{:S(2)}, u32[]{:S(2)}) collective-permute-start(bf16[4,4,64,128]{3,2,1,0:T(8,128)(2,1)S(1)} %pad_maximum_fusion.refs_0_), channel_id=1, source_target_pairs={{0,24},{1,25},{2,26},{3,27},{4,28},{5,29},{6,30},{7,31},{8,0},{9,1... | collective-permute-start | bytes 786440 | tf_op jit(solution)/shard_map/ppermute | solution.py:279
  25.7 8.4 %collective-permute-start.5 = (bf16[4,4,64,128]{3,2,1,0:T(8,128)(2,1)S(1)}, bf16[4,4,64,128]{3,2,1,0:T(8,128)(2,1)S(1)}, u32[]{:S(2)}, u32[]{:S(2)}) collective-permute-start(bf16[4,4,64,128]{3,2,1,0:T(8,128)(2,1)S(1)} %pad_maximum_fusion.refs_0_), channel_id=1, source_target_pairs={{0,16},{1,17},{2,18},{3,19},{4,20},{5,21},{6,22},{7,23},{8,24},{9,... | collective-permute-start | bytes 786440 | tf_op jit(solution)/shard_map/ppermute | solution.py:279
  34.6 8.9 %collective-permute-start.9 = (bf16[2,128,128]{2,1,0:T(8,128)(2,1)S(1)}, bf16[2,128,128]{2,1,0:T(8,128)(2,1)S(1)}, u32[]{:S(2)}, u32[]{:S(2)}) collective-permute-start(bf16[2,128,128]{2,1,0:T(8,128)(2,1)S(1)} %apply.7), channel_id=1, source_target_pairs={{0,1},{1,0},{2,3},{3,2},{4,5},{5,4},{6,7},{7,6},{8,9},{9,8},{10,11... | collective-permute-start | bytes 196616 | tf_op jit(solution)/shard_map/ppermute | solution.py:279

commit v4 on v3

--- a/solution.py
+++ b/solution.py
@@ -215,7 +215,7 @@
                     cos_cols.append(jnp.concatenate(real + imag, axis=0))
                     sin_cols.append(jnp.concatenate([-v for v in imag] + real, axis=0))
                 columns = jnp.concatenate(cos_cols + sin_cols, axis=1).astype(jnp.bfloat16)
-                table, p = pairs[start + 2 * i + q]
+                table, p = pairs[2 * start[i] + q]
                 product = lax.dot_general(
                     table[p, f],
                     columns,
@@ -307,11 +307,11 @@
     planes = [line]
     for d in SHIFTS:
         planes.append(send(line, second(d)))
-    theirs = apply_tables(planes[:1], (partner,), 0, None, None)
-    theirs = apply_tables(planes[2:], (partner,), 4, theirs, None)
-    theirs = apply_tables(planes[1:2], (partner,), 2, theirs, jnp.bfloat16)
+    early = (planes[0], planes[2], planes[3])
+    theirs = apply_tables(early, (partner,), (0, 2, 3), None, None)
+    theirs = apply_tables(planes[1:2], (partner,), (1,), theirs, jnp.bfloat16)
     theirs = send(theirs, lambda zh, c, y, x, zl: (zh, c, y, x, 1 - zl))
-    mine = apply_tables(planes, own, 0, None, jnp.float32)
+    mine = apply_tables(planes, own, (0, 1, 2, 3), None, jnp.float32)
     seg_count = samples.shape[0] * lax.axis_size("tm")
     return powers(mine, theirs, 1.0 / (delays.shape[1] * seg_count))
 

time: 44.3 us -> 44.3 us (level)
    pallas_call x4 -> x3, Pallas kernels: 2.89 us -> 2.74 us  [apply_tables(): pl.pallas_call(lambda *refs: apply_kernel(len(planes), len(tables), start...]
where the time goes in v4:
time: 44.3 us; the launch traced here: 44.1 us
  Pallas kernels  19.5 us (44%)
  starting transfers between devices  15.9 us (36%)
  waiting for transfers between devices  8.5 us (19%)
    ppermute x10, starting transfers between devices, send(): return lax.ppermute(value, AXES, route(move))  15.9 us
    pallas_call x4, Pallas kernels, steer_tables(): pl.pallas_call(lambda *refs: steer_kernel(start, len(delays) == 2, *refs)...  10 us
    ppermute x10, waiting for transfers between devices, send(): return lax.ppermute(value, AXES, route(move))  8.5 us
    pallas_call x1, Pallas kernels, transform(): pl.pallas_call(transform_kernel, in_specs=[pl.BlockSpec(memory_space=pltp...  6.11 us
    pallas_call x3, Pallas kernels, apply_tables(): pl.pallas_call(lambda *refs: apply_kernel(len(planes), len(tables), start...  2.74 us
  transfers between devices with their start and end apart: 10, of which 5 were waited for; matrix products, arithmetic and copies ran while one was open for 0% of the time, Pallas kernels for 28%

profile of v4, /device:TPU:6, one launch (start us, length us, event | category | flops | bytes accessed | tf_op | source)
XLA Modules:
  0.0 44.1 jit_solution(9888715500444410538)
XLA Ops:
  0.0 0.0 copy-start
  0.0 6.1 %transform.1 = (bf16[2,64,128]{2,1,0:T(8,128)(2,1)S(1)}, bf16[2,64,128]{2,1,0:T(8,128)(2,1)S(1)}, s16[16,128,128]{2,1,0:T(8,128)(2,1)S(1)}, s16[16,128,128]{2,1,0:T(8,128)(2,1)S(1)}) custom-call(s32[16]{0:T(128)} %refs_0_.7, s32[128,4096]{1,0:T(8,128)} %delays_in.1, bf16[8,128,4096]{2,1,0:T(8,128)(2,1)} %samples.1), custom_call_target="tpu_custom_call" | custom-call | tf_op jit(solution)/shard_map/transform/pallas_call | solution.py:121
  6.1 0.1 collective-permute-start
  6.2 1.2 %collective-permute-done = bf16[2,64,128]{2,1,0:T(8,128)(2,1)S(1)} collective-permute-done((bf16[2,64,128]{2,1,0:T(8,128)(2,1)S(1)}, bf16[2,64,128]{2,1,0:T(8,128)(2,1)S(1)}, u32[]{:S(2)}, u32[]{:S(2)}) %collective-permute-start) | collective-permute-done | bytes 32800 | tf_op jit(solution)/shard_map/ppermute | solution.py:279
  7.4 4.0 %collective-permute-start.1 = (bf16[2,64,128]{2,1,0:T(8,128)(2,1)S(1)}, bf16[2,64,128]{2,1,0:T(8,128)(2,1)S(1)}, u32[]{:S(2)}, u32[]{:S(2)}) collective-permute-start(bf16[2,64,128]{2,1,0:T(8,128)(2,1)S(1)} %pad_maximum_fusion.2), channel_id=1, source_target_pairs={{0,64},{1,65},{2,66},{3,67},{4,68},{5,69},{6,70},{7,71},{8,72},{9,... | collective-permute-start | bytes 98312 | tf_op jit(solution)/shard_map/ppermute | solution.py:279
  11.4 1.0 %collective-permute-start.8 = (s16[16,128,128]{2,1,0:T(8,128)(2,1)S(1)}, s16[16,128,128]{2,1,0:T(8,128)(2,1)S(1)}, u32[]{:S(2)}, u32[]{:S(2)}) collective-permute-start(s16[16,128,128]{2,1,0:T(8,128)(2,1)S(1)} %get-tuple-element.12), channel_id=1, source_target_pairs={{0,1},{1,0},{2,3},{3,2},{4,5},{5,4},{6,7},{7,6},{8,9},{9,8},{10,11... | collective-permute-start | bytes 1572872 | tf_op jit(solution)/shard_map/ppermute | solution.py:279
  12.4 0.9 %collective-permute-done.1 = bf16[2,64,128]{2,1,0:T(8,128)(2,1)S(1)} collective-permute-done((bf16[2,64,128]{2,1,0:T(8,128)(2,1)S(1)}, bf16[2,64,128]{2,1,0:T(8,128)(2,1)S(1)}, u32[]{:S(2)}, u32[]{:S(2)}) %collective-permute-start.1) | collective-permute-done | bytes 32800 | tf_op jit(solution)/shard_map/ppermute | solution.py:279
  13.3 1.5 %collective-permute-start.2 = (bf16[4,64,128]{2,1,0:T(8,128)(2,1)S(1)}, bf16[4,64,128]{2,1,0:T(8,128)(2,1)S(1)}, u32[]{:S(2)}, u32[]{:S(2)}) collective-permute-start(bf16[4,64,128]{2,1,0:T(8,128)(2,1)S(1)} %get-tuple-element.14), channel_id=1, source_target_pairs={{0,4},{1,5},{2,6},{3,7},{4,0},{5,1},{6,2},{7,3},{8,12},{9,13},{10,... | collective-permute-start | bytes 196616 | tf_op jit(solution)/shard_map/ppermute | solution.py:279
  14.8 2.1 %collective-permute-start.3 = (bf16[4,64,128]{2,1,0:T(8,128)(2,1)S(1)}, bf16[4,64,128]{2,1,0:T(8,128)(2,1)S(1)}, u32[]{:S(2)}, u32[]{:S(2)}) collective-permute-start(bf16[4,64,128]{2,1,0:T(8,128)(2,1)S(1)} %get-tuple-element.14), channel_id=1, source_target_pairs={{0,2},{1,3},{2,4},{3,5},{4,6},{5,7},{6,0},{7,1},{8,10},{9,11},{10,... | collective-permute-start | bytes 196616 | tf_op jit(solution)/shard_map/ppermute | solution.py:279
  16.9 0.0 collective-permute-start.4
  16.9 2.3 %collective-permute-done.2 = bf16[4,64,128]{2,1,0:T(8,128)(2,1)S(1)} collective-permute-done((bf16[4,64,128]{2,1,0:T(8,128)(2,1)S(1)}, bf16[4,64,128]{2,1,0:T(8,128)(2,1)S(1)}, u32[]{:S(2)}, u32[]{:S(2)}) %collective-permute-start.2) | collective-permute-done | bytes 65568 | tf_op jit(solution)/shard_map/ppermute | solution.py:279
  19.1 0.0 collective-permute-done.3
  19.1 3.2 %collective-permute-done.4 = bf16[4,64,128]{2,1,0:T(8,128)(2,1)S(1)} collective-permute-done((bf16[4,64,128]{2,1,0:T(8,128)(2,1)S(1)}, bf16[4,64,128]{2,1,0:T(8,128)(2,1)S(1)}, u32[]{:S(2)}, u32[]{:S(2)}) %collective-permute-start.4) | collective-permute-done | bytes 65568 | tf_op jit(solution)/shard_map/ppermute | solution.py:279
  22.4 1.6 %collective-permute-start.6 = (bf16[4,4,64,128]{3,2,1,0:T(8,128)(2,1)S(1)}, bf16[4,4,64,128]{3,2,1,0:T(8,128)(2,1)S(1)}, u32[]{:S(2)}, u32[]{:S(2)}) collective-permute-start(bf16[4,4,64,128]{3,2,1,0:T(8,128)(2,1)S(1)} %pad_maximum_fusion.refs_0_), channel_id=1, source_target_pairs={{0,8},{1,9},{2,10},{3,11},{4,12},{5,13},{6,14},{7,15},{8,16},{9,17... | collective-permute-start | bytes 786440 | tf_op jit(solution)/shard_map/ppermute | solution.py:279
  24.0 1.7 %collective-permute-start.7 = (bf16[4,4,64,128]{3,2,1,0:T(8,128)(2,1)S(1)}, bf16[4,4,64,128]{3,2,1,0:T(8,128)(2,1)S(1)}, u32[]{:S(2)}, u32[]{:S(2)}) collective-permute-start(bf16[4,4,64,128]{3,2,1,0:T(8,128)(2,1)S(1)} %pad_maximum_fusion.refs_0_), channel_id=1, source_target_pairs={{0,24},{1,25},{2,26},{3,27},{4,28},{5,29},{6,30},{7,31},{8,0},{9,1... | collective-permute-start | bytes 786440 | tf_op jit(solution)/shard_map/ppermute | solution.py:279
  25.7 2.0 %collective-permute-start.5 = (bf16[4,4,64,128]{3,2,1,0:T(8,128)(2,1)S(1)}, bf16[4,4,64,128]{3,2,1,0:T(8,128)(2,1)S(1)}, u32[]{:S(2)}, u32[]{:S(2)}) collective-permute-start(bf16[4,4,64,128]{3,2,1,0:T(8,128)(2,1)S(1)} %pad_maximum_fusion.refs_0_), channel_id=1, source_target_pairs={{0,16},{1,17},{2,18},{3,19},{4,20},{5,21},{6,22},{7,23},{8,24},{9,... | collective-permute-start | bytes 786440 | tf_op jit(solution)/shard_map/ppermute | solution.py:279
  27.7 0.0 collective-permute-done.8.refs_1_
  27.7 0.0 copy-done
  27.7 4.4 %steer.7.refs_3_.refs_1_ = bf16[8,4,128,512]{3,2,1,0:T(8,128)(2,1)S(1)} custom-call(s32[16]{0:T(128)S(1)} %copy-done, s16[16,128,128]{2,1,0:T(8,128)(2,1)S(1)} %collective-permute-done.8.refs_1_), custom_call_target="tpu_custom_call" | custom-call | tf_op jit(solution)/shard_map/steer/pallas_call | solution.py:186
  32.1 0.0 collective-permute-done.6.refs_2_.refs_1_
  32.1 0.0 collective-permute-done.7.refs_3_.refs_2_
  32.2 1.0 %apply.4.refs_2_ = f32[4,128,64]{2,1,0:T(8,128)S(1)} custom-call(bf16[4,4,64,128]{3,2,1,0:T(8,128)(2,1)S(1)} %pad_maximum_fusion.refs_0_, bf16[4,4,64,128]{3,2,1,0:T(8,128)(2,1)S(1)} %collective-permute-done.6.refs_2_.refs_1_, bf16[4,4,64,128]{3,2,1,0:T(8,128)(2,1)S(1)} %collective-permute-done.7.refs_3_.refs_2_, ...), custom_call_target="tpu_custom_call" | custom-call | tf_op jit(solution)/shard_map/apply/pallas_call | solution.py:236
  33.1 1.0 %collective-permute-done.5.refs_1_.refs_0_ = bf16[4,4,64,128]{3,2,1,0:T(8,128)(2,1)S(1)} collective-permute-done((bf16[4,4,64,128]{3,2,1,0:T(8,128)(2,1)S(1)}, bf16[4,4,64,128]{3,2,1,0:T(8,128)(2,1)S(1)}, u32[]{:S(2)}, u32[]{:S(2)}) %collective-permute-start.5) | collective-permute-done | bytes 262176 | tf_op jit(solution)/shard_map/ppermute | solution.py:279
  34.1 0.5 %apply.5 = bf16[2,128,128]{2,1,0:T(8,128)(2,1)S(1)} custom-call(bf16[4,4,64,128]{3,2,1,0:T(8,128)(2,1)S(1)} %collective-permute-done.5.refs_1_.refs_0_, bf16[8,4,128,512]{3,2,1,0:T(8,128)(2,1)S(1)} %steer.7.refs_3_.refs_1_, f32[4,128,64]{2,1,0:T(8,128)S(1)} %apply.4.refs_2_), custom_call_target="tpu_custom_call" | custom-call | tf_op jit(solution)/shard_map/apply/pallas_call | solution.py:236
  34.6 2.0 %collective-permute-start.9 = (bf16[2,128,128]{2,1,0:T(8,128)(2,1)S(1)}, bf16[2,128,128]{2,1,0:T(8,128)(2,1)S(1)}, u32[]{:S(2)}, u32[]{:S(2)}) collective-permute-start(bf16[2,128,128]{2,1,0:T(8,128)(2,1)S(1)} %apply.5), channel_id=1, source_target_pairs={{0,1},{1,0},{2,3},{3,2},{4,5},{5,4},{6,7},{7,6},{8,9},{9,8},{10,11... | collective-permute-start | bytes 196616 | tf_op jit(solution)/shard_map/ppermute | solution.py:279
  36.6 2.5 %steer.5.refs_5_ = bf16[4,4,128,512]{3,2,1,0:T(8,128)(2,1)S(1)} custom-call(s32[16]{0:T(128)S(1)} %copy-done, s16[16,128,128]{2,1,0:T(8,128)(2,1)S(1)} %get-tuple-element.11.refs_1_), custom_call_target="tpu_custom_call" | custom-call | tf_op jit(solution)/shard_map/steer/pallas_call | solution.py:186
  39.1 1.5 %steer.4.refs_4_ = bf16[2,4,128,512]{3,2,1,0:T(8,128)(2,1)S(1)} custom-call(s32[16]{0:T(128)S(1)} %copy-done, s16[16,128,128]{2,1,0:T(8,128)(2,1)S(1)} %get-tuple-element.11.refs_1_), custom_call_target="tpu_custom_call" | custom-call | tf_op jit(solution)/shard_map/steer/pallas_call | solution.py:186
  40.6 1.5 %steer.6.refs_6_ = bf16[2,4,128,512]{3,2,1,0:T(8,128)(2,1)S(1)} custom-call(s32[16]{0:T(128)S(1)} %copy-done, s16[16,128,128]{2,1,0:T(8,128)(2,1)S(1)} %get-tuple-element.11.refs_1_), custom_call_target="tpu_custom_call" | custom-call | tf_op jit(solution)/shard_map/steer/pallas_call | solution.py:186
  42.1 1.3 %apply.3.refs_0_ = f32[2,128,128]{2,1,0:T(8,128)S(1)} custom-call(bf16[4,4,64,128]{3,2,1,0:T(8,128)(2,1)S(1)} %pad_maximum_fusion.refs_0_, bf16[4,4,64,128]{3,2,1,0:T(8,128)(2,1)S(1)} %collective-permute-done.5.refs_1_.refs_0_, bf16[4,4,64,128]{3,2,1,0:T(8,128)(2,1)S(1)} %collective-permute-done.6.refs_2_.refs_1_, ...), custom_call_target="tpu_custom_call" | custom-call | tf_op jit(solution)/shard_map/apply/pallas_call | solution.py:236
  43.4 0.0 collective-permute-done.9.refs_1_
  43.5 0.7 %powers.1 = f32[4,128]{1,0:T(4,128)} custom-call(f32[2,128,128]{2,1,0:T(8,128)S(1)} %apply.3.refs_0_, bf16[2,128,128]{2,1,0:T(8,128)(2,1)S(1)} %collective-permute-done.9.refs_1_), custom_call_target="tpu_custom_call" | custom-call | tf_op jit(solution)/shard_map/powers/pallas_call | solution.py:258
  (5 shorter events, 0.1 us)
Async XLA Ops:
  0.0 27.7 %copy-start = (s32[16]{0:T(128)S(1)}, s32[16]{0:T(128)}, u32[]{:S(2)}) copy-start(s32[16]{0:T(128)} %refs_0_.7) | copy-start | bytes 196
  6.1 1.3 %collective-permute-start = (bf16[2,64,128]{2,1,0:T(8,128)(2,1)S(1)}, bf16[2,64,128]{2,1,0:T(8,128)(2,1)S(1)}, u32[]{:S(2)}, u32[]{:S(2)}) collective-permute-start(bf16[2,64,128]{2,1,0:T(8,128)(2,1)S(1)} %get-tuple-element.10), channel_id=1, source_target_pairs={{0,32},{1,33},{2,34},{3,35},{4,36},{5,37},{6,38},{7,39},{8,40},{9,... | collective-permute-start | bytes 98312 | tf_op jit(solution)/shard_map/ppermute | solution.py:279
  7.4 5.9 %collective-permute-start.1 = (bf16[2,64,128]{2,1,0:T(8,128)(2,1)S(1)}, bf16[2,64,128]{2,1,0:T(8,128)(2,1)S(1)}, u32[]{:S(2)}, u32[]{:S(2)}) collective-permute-start(bf16[2,64,128]{2,1,0:T(8,128)(2,1)S(1)} %pad_maximum_fusion.2), channel_id=1, source_target_pairs={{0,64},{1,65},{2,66},{3,67},{4,68},{5,69},{6,70},{7,71},{8,72},{9,... | collective-permute-start | bytes 98312 | tf_op jit(solution)/shard_map/ppermute | solution.py:279
  11.4 16.3 %collective-permute-start.8 = (s16[16,128,128]{2,1,0:T(8,128)(2,1)S(1)}, s16[16,128,128]{2,1,0:T(8,128)(2,1)S(1)}, u32[]{:S(2)}, u32[]{:S(2)}) collective-permute-start(s16[16,128,128]{2,1,0:T(8,128)(2,1)S(1)} %get-tuple-element.12), channel_id=1, source_target_pairs={{0,1},{1,0},{2,3},{3,2},{4,5},{5,4},{6,7},{7,6},{8,9},{9,8},{10,11... | collective-permute-start | bytes 1572872 | tf_op jit(solution)/shard_map/ppermute | solution.py:279
  13.3 5.8 %collective-permute-start.2 = (bf16[4,64,128]{2,1,0:T(8,128)(2,1)S(1)}, bf16[4,64,128]{2,1,0:T(8,128)(2,1)S(1)}, u32[]{:S(2)}, u32[]{:S(2)}) collective-permute-start(bf16[4,64,128]{2,1,0:T(8,128)(2,1)S(1)} %get-tuple-element.14), channel_id=1, source_target_pairs={{0,4},{1,5},{2,6},{3,7},{4,0},{5,1},{6,2},{7,3},{8,12},{9,13},{10,... | collective-permute-start | bytes 196616 | tf_op jit(solution)/shard_map/ppermute | solution.py:279
  14.8 4.4 %collective-permute-start.3 = (bf16[4,64,128]{2,1,0:T(8,128)(2,1)S(1)}, bf16[4,64,128]{2,1,0:T(8,128)(2,1)S(1)}, u32[]{:S(2)}, u32[]{:S(2)}) collective-permute-start(bf16[4,64,128]{2,1,0:T(8,128)(2,1)S(1)} %get-tuple-element.14), channel_id=1, source_target_pairs={{0,2},{1,3},{2,4},{3,5},{4,6},{5,7},{6,0},{7,1},{8,10},{9,11},{10,... | collective-permute-start | bytes 196616 | tf_op jit(solution)/shard_map/ppermute | solution.py:279
  16.9 5.5 %collective-permute-start.4 = (bf16[4,64,128]{2,1,0:T(8,128)(2,1)S(1)}, bf16[4,64,128]{2,1,0:T(8,128)(2,1)S(1)}, u32[]{:S(2)}, u32[]{:S(2)}) collective-permute-start(bf16[4,64,128]{2,1,0:T(8,128)(2,1)S(1)} %get-tuple-element.14), channel_id=1, source_target_pairs={{0,6},{1,7},{2,0},{3,1},{4,2},{5,3},{6,4},{7,5},{8,14},{9,15},{10,... | collective-permute-start | bytes 196616 | tf_op jit(solution)/shard_map/ppermute | solution.py:279
  22.4 9.8 %collective-permute-start.6 = (bf16[4,4,64,128]{3,2,1,0:T(8,128)(2,1)S(1)}, bf16[4,4,64,128]{3,2,1,0:T(8,128)(2,1)S(1)}, u32[]{:S(2)}, u32[]{:S(2)}) collective-permute-start(bf16[4,4,64,128]{3,2,1,0:T(8,128)(2,1)S(1)} %pad_maximum_fusion.refs_0_), channel_id=1, source_target_pairs={{0,8},{1,9},{2,10},{3,11},{4,12},{5,13},{6,14},{7,15},{8,16},{9,17... | collective-permute-start | bytes 786440 | tf_op jit(solution)/shard_map/ppermute | solution.py:279
  24.0 8.1 %collective-permute-start.7 = (bf16[4,4,64,128]{3,2,1,0:T(8,128)(2,1)S(1)}, bf16[4,4,64,128]{3,2,1,0:T(8,128)(2,1)S(1)}, u32[]{:S(2)}, u32[]{:S(2)}) collective-permute-start(bf16[4,4,64,128]{3,2,1,0:T(8,128)(2,1)S(1)} %pad_maximum_fusion.refs_0_), channel_id=1, source_target_pairs={{0,24},{1,25},{2,26},{3,27},{4,28},{5,29},{6,30},{7,31},{8,0},{9,1... | collective-permute-start | bytes 786440 | tf_op jit(solution)/shard_map/ppermute | solution.py:279
  25.7 8.4 %collective-permute-start.5 = (bf16[4,4,64,128]{3,2,1,0:T(8,128)(2,1)S(1)}, bf16[4,4,64,128]{3,2,1,0:T(8,128)(2,1)S(1)}, u32[]{:S(2)}, u32[]{:S(2)}) collective-permute-start(bf16[4,4,64,128]{3,2,1,0:T(8,128)(2,1)S(1)} %pad_maximum_fusion.refs_0_), channel_id=1, source_target_pairs={{0,16},{1,17},{2,18},{3,19},{4,20},{5,21},{6,22},{7,23},{8,24},{9,... | collective-permute-start | bytes 786440 | tf_op jit(solution)/shard_map/ppermute | solution.py:279
  34.6 8.9 %collective-permute-start.9 = (bf16[2,128,128]{2,1,0:T(8,128)(2,1)S(1)}, bf16[2,128,128]{2,1,0:T(8,128)(2,1)S(1)}, u32[]{:S(2)}, u32[]{:S(2)}) collective-permute-start(bf16[2,128,128]{2,1,0:T(8,128)(2,1)S(1)} %apply.5), channel_id=1, source_target_pairs={{0,1},{1,0},{2,3},{3,2},{4,5},{5,4},{6,7},{7,6},{8,9},{9,8},{10,11... | collective-permute-start | bytes 196616 | tf_op jit(solution)/shard_map/ppermute | solution.py:279
